TPU v7x, 32 devices: a whole 2x2x4 slice. The times are simulated.
32 devices in a mesh: date: 16 (over z, y, core), strip: 2 (over x).
Axes of the slice: x: 2, y: 2, z: 4, core: 2. Of those that a mesh axis runs over, the one named last changes fastest.
Arguments:
- acquisitions: bfloat16 [32, 2, 2, 344, 640], P('date', None, None, None, 'strip'), may hold values from -6 to 6
- shifts: int32 [2, 32, 2, 5, 10], P(None, 'date', None, None, 'strip'), may hold values from -8 to 8, as said below
- fractions: int32 [2, 32, 2, 5, 10], P(None, 'date', None, None, 'strip'), may hold values from 0 to 63
- ref_dates: int32 [2], replicated, may hold values from 0 to 31, as said below
Outputs:
- chip_corr: float32 [2, 32, 2, 5, 10], P(None, 'date', None, None, 'strip')
- coherence: float32 [2, 31, 2, 64, 32], P(None, None, None, 'date', 'strip')
Inputs may be any that keep to these rules, and one draw needn't show every extreme that they name: `shifts`: zero at every chip of date ref_dates[t] in tile t. `ref_dates`: the reference dates of consecutive tiles lie in different blocks of 2 dates.
All inputs are finite; a program needn't handle non-finite values.
Results may differ from a plain program's by a relative error of at most 0.0021.
Values may be sent and summed in bfloat16 or wider, within the bound.
A program may use at most 64 MiB of HBM per device.

v0:
```python
import jax
import jax.numpy as jnp
from jax import lax
from jax.sharding import PartitionSpec as P

TILE_COUNT = 2
CHIP_SIZE = 64
TAP_COUNT = 8
SUBSTEPS = 64
LOOK_AZ = 5
LOOK_RG = 20
MARGIN = 12


epsilon = 1e-06


def padded_2(block, sides, width):
    for axis, dim in sides:
        count = lax.axis_size(axis)
        forward = [(i, i + 1) for i in range(count - 1)]
        backward = [(target, source) for source, target in forward]
        low = lax.ppermute(
            lax.slice_in_dim(block, block.shape[dim] - width, None, axis=dim), axis, forward
        )
        high = lax.ppermute(lax.slice_in_dim(block, 0, width, axis=dim), axis, backward)
        block = jnp.concatenate([low, block, high], axis=dim)
    return block


def spread(value, axis, source):
    kept = jnp.where(lax.axis_index(axis) == source, value, 0).astype(value.dtype)
    return lax.psum(kept, axis)


def passed_along(block, axis, distance):
    devices = range(lax.axis_size(axis))
    route = [(i - distance, i) for i in devices if i - distance in devices]
    return lax.ppermute(block, axis, route)


def sinc_matrix(shift_part, fraction_part):
    window_size = CHIP_SIZE + 2 * MARGIN
    offset = fraction_part.astype(jnp.float32) / SUBSTEPS
    tap_axis = jnp.arange(TAP_COUNT).astype(jnp.float32)
    distance = tap_axis - (TAP_COUNT // 2 - 1) - offset[..., None]
    weights = jnp.sinc(distance) * (0.5 + 0.5 * jnp.cos(jnp.pi * distance / (TAP_COUNT // 2)))
    weights = weights / jnp.sum(weights, axis=-1, keepdims=True)
    out_rows = jnp.arange(CHIP_SIZE, dtype=jnp.int32)[:, None]
    in_rows = jnp.arange(window_size, dtype=jnp.int32)[None, :]
    matrix = jnp.zeros(shift_part.shape + (CHIP_SIZE, window_size), jnp.float32)
    for tap_index in range(TAP_COUNT):
        target = out_rows + shift_part[..., None, None] + (tap_index - TAP_COUNT // 2 + 1 + MARGIN)
        matrix = matrix + jnp.where(
            in_rows == target, weights[..., tap_index][..., None, None], 0.0
        )
    return matrix.astype(jnp.bfloat16)


def correlate(reference_tiles, resampled):
    chips_az = resampled.shape[-2] // CHIP_SIZE
    chips_rg = resampled.shape[-1] // CHIP_SIZE

    def as_chips(values):
        return values.astype(jnp.float32).reshape(
            values.shape[:-2] + (chips_az, CHIP_SIZE, chips_rg, CHIP_SIZE)
        )

    ref_chips = as_chips(reference_tiles)
    sec_chips = as_chips(resampled)
    ref_real = ref_chips[..., 0, :, :, :, :]
    ref_imag = ref_chips[..., 1, :, :, :, :]
    sec_real = sec_chips[..., 0, :, :, :, :]
    sec_imag = sec_chips[..., 1, :, :, :, :]
    cross_real = jnp.sum(ref_real * sec_real + ref_imag * sec_imag, axis=(-3, -1))
    cross_imag = jnp.sum(ref_imag * sec_real - ref_real * sec_imag, axis=(-3, -1))
    ref_power = jnp.sum(ref_real * ref_real + ref_imag * ref_imag, axis=(-3, -1))
    sec_power = jnp.sum(sec_real * sec_real + sec_imag * sec_imag, axis=(-3, -1))
    denominator = jnp.sqrt((ref_power + epsilon) * (sec_power + epsilon))
    return jnp.stack([cross_real / denominator, cross_imag / denominator])


def multilook_pairs(series):
    values = series.astype(jnp.float32)
    earlier = values[:-1]
    second = values[1:]
    early_real = earlier[:, :, 0]
    early_imag = earlier[:, :, 1]
    later_real = second[:, :, 0]
    later_imag = second[:, :, 1]
    cross_real = early_real * later_real + early_imag * later_imag
    cross_imag = early_imag * later_real - early_real * later_imag
    power_early = early_real * early_real + early_imag * early_imag
    power_later = later_real * later_real + later_imag * later_imag

    def box_sum(quantity):
        blocked = quantity.reshape(
            quantity.shape[:2]
            + (quantity.shape[2] // LOOK_AZ, LOOK_AZ, quantity.shape[3] // LOOK_RG, LOOK_RG)
        )
        return jnp.sum(blocked, axis=(3, 5))

    denominator = jnp.sqrt((box_sum(power_early) + epsilon) * (box_sum(power_later) + epsilon))
    return jnp.stack([box_sum(cross_real) / denominator, box_sum(cross_imag) / denominator])


def resample(padded, shift_part, fraction_part):
    window_size = CHIP_SIZE + 2 * MARGIN
    chips_az = shift_part.shape[3]
    chips_rg = shift_part.shape[4]
    pieces = [
        padded[
            :,
            :,
            :,
            chip_row * CHIP_SIZE : chip_row * CHIP_SIZE + window_size,
            chip_col * CHIP_SIZE : chip_col * CHIP_SIZE + window_size,
        ]
        for chip_row in range(chips_az)
        for chip_col in range(chips_rg)
    ]
    windows = jnp.stack(pieces, axis=3).reshape(
        padded.shape[:3] + (chips_az, chips_rg, window_size, window_size)
    )
    azimuth = sinc_matrix(shift_part[0], fraction_part[0])
    across = sinc_matrix(shift_part[1], fraction_part[1])
    partial_rows = jnp.einsum(
        "dtariw,dtcarwv->dtcariv", azimuth, windows, preferred_element_type=jnp.float32
    ).astype(jnp.bfloat16)
    chips_out = jnp.einsum(
        "dtcariv,dtarjv->dtcarij", partial_rows, across, preferred_element_type=jnp.float32
    ).astype(jnp.bfloat16)
    return chips_out.transpose(0, 1, 2, 3, 5, 4, 6).reshape(
        padded.shape[:3] + (chips_az * CHIP_SIZE, chips_rg * CHIP_SIZE)
    )


def per_device(acquisitions, shifts, fractions, ref_dates):
    dates_local = acquisitions.shape[0]
    tile_rows = acquisitions.shape[3] - 2 * MARGIN
    padded = padded_2(acquisitions, (("strip", 4),), MARGIN)
    owners = ref_dates // dates_local
    slots = ref_dates % dates_local
    candidates = [
        lax.dynamic_index_in_dim(acquisitions[:, tile_index], slots[tile_index], 0, keepdims=False)[
            :, MARGIN : MARGIN + tile_rows, :
        ]
        for tile_index in range(TILE_COUNT)
    ]
    reference_tiles = jnp.stack(
        [
            spread(candidates[tile_index], "date", owners[tile_index])
            for tile_index in range(TILE_COUNT)
        ]
    )
    resampled = resample(padded, shifts, fractions)
    chip_corr = correlate(reference_tiles, resampled)
    following = passed_along(resampled[0:1], "date", -1)
    series = jnp.concatenate([resampled, following], axis=0)
    looked = multilook_pairs(series)
    regrouped = lax.all_to_all(looked, "date", split_axis=3, concat_axis=1, tiled=True)
    coherence = regrouped[:, : dates_local * lax.axis_size("date") - 1]
    return (chip_corr, coherence)


def solution(mesh):
    return jax.shard_map(
        per_device,
        mesh=mesh,
        in_specs=(
            P("date", None, None, None, "strip"),
            P(None, "date", None, None, "strip"),
            P(None, "date", None, None, "strip"),
            P(),
        ),
        out_specs=(P(None, "date", None, None, "strip"), P(None, None, None, "date", "strip")),
        check_vma=False,
    )
```

profile of v0, /device:TPU:0, one launch (start us, length us, event | category | flops | bytes accessed | tf_op | source)
XLA Modules:
  0.0 226.9 jit_solution(10947532881645513688)
XLA Ops:
  7.2 1.0 fusion.119
  8.2 1.3 collective-permute-start.1
  9.5 4.9 %collective-permute-start = (bf16[2,2,2,344,12]{3,4,2,1,0:T(8,128)(2,1)S(1)}, bf16[2,2,2,344,12]{3,4,2,1,0:T(8,128)(2,1)S(1)}, u32[]{:S(2)}, u32[]{:S(2)}) collective-permute-start(bf16[2,2,2,344,12]{3,4,2,1,0:T(8,128)(2,1)S(1)} %get-tuple-element.29), channel_id=1, source_target_pairs={{0,1},{2,3},{4,5},{6,7},{8,9},{10,11},{12,13},{14,15},{16,17},{18,... | collective-permute-start | bytes 198152 | tf_op jit(solution)/shard_map/ppermute | solution.py:23
  18.2 1.7 fusion.118
  23.6 1.6 stack.98
  25.2 1.6 stack.97
  26.9 3.2 %fusion.114 = (f32[2,2,5,5]{3,1,2,0:T(2,128)S(1)}, f32[2,2,5,5]{3,1,2,0:T(2,128)S(1)}) fusion(f32[2,2,5,5]{3,1,2,0:T(2,128)S(1)} %get-tuple-element.53, f32[8]{0:T(128)S(1)} %convert_add_fusion, f32[2,2,5,5]{3,1,2,0:T(2,128)S(1)} %get-tuple-element.52), kind=kLoop, calls=%fused_computation.187 | loop fusion | flops 62200 | bytes 1632 | tf_op jit(solution)/shard_map/reduce_sum | solution.py:48
  30.1 3.1 %broadcast_divide_fusion.1 = (f32[2,2,5,5,8]{3,1,2,0,4:T(2,128)S(1)}, f32[2,2,5,5,8]{3,1,2,0,4:T(2,128)S(1)}) fusion(f32[2,2,5,5]{3,1,2,0:T(2,128)S(1)} %get-tuple-element.16, f32[2,2,5,5]{3,1,2,0:T(2,128)S(1)} %get-tuple-element.53, f32[8]{0:T(128)S(1)} %convert_add_fusion, f32[2,2,5,5]{3,1,2,0:T(2,128)S(1)} %get-tuple-element.17, ...), kind=kLoop, calls=%fused_computation.185 | loop fusion | flops 62400 | bytes 8032 | tf_op jit(solution)/shard_map/div | solution.py:48
  33.2 0.9 fusion.104
  42.3 0.8 fusion.70
  43.2 0.8 bitcast_dynamic-update-slice_fusion.11
  44.0 0.8 bitcast_dynamic-update-slice_fusion.10
  44.8 0.8 bitcast_dynamic-update-slice_fusion.9
  45.7 0.8 fusion.69
  50.1 0.9 fusion.66
  51.0 0.8 bitcast_dynamic-update-slice_fusion.5
  51.8 0.8 bitcast_dynamic-update-slice_fusion.4
  52.7 0.8 bitcast_dynamic-update-slice_fusion.3
  53.5 0.8 fusion.65
  58.0 7.2 %copy.165 = bf16[2,2,2,25,88,88]{5,4,2,3,1,0:T(8,128)(2,1)} copy(bf16[2,2,2,25,88,88]{4,5,2,1,0,3:T(8,128)(2,1)} %fusion.62) | data formatting | bytes 6195200 | tf_op jit(solution)/shard_map/stack | solution.py:122
  65.4 13.2 %fusion.4.clone.5 = bf16[2,2,2,5,5,64,88]{6,5,2,4,3,1,0:T(8,128)(2,1)S(1)} fusion(bf16[2,2,2,5,5,88,88]{6,5,2,4,3,1,0:T(8,128)(2,1)} %bitcast.221, f32[2,2,5,5]{3,2,1,0:T(8,128)S(1)} %copy.174, s32[2,2,5,5,64]{4,3,2,1,0:T(8,128)S(1)} %get-tuple-element.63, f32[2,2,5,5]{3,2,1,0:T(8,128)S(1)} %copy.173, ...), kind=kOutput, calls=%fused_computation.3.clone.clone.clone.clone.clone.2 | convolution fusion | flops 212889600 | bytes 5558400 | tf_op jit(solution)/shard_map/dtariw,dtcarwv->dtcariv/dot_general | solution.py:127
  78.7 13.6 %fusion.122 = (f32[2,2,2,5,64,5,64]{4,6,2,5,3,1,0:T(8,128)}, bf16[2,2,2,5,64,5,64]{4,6,2,5,3,1,0:T(8,128)(2,1)S(1)}) fusion(f32[2,2,5,5]{3,2,1,0:T(8,128)S(1)} %copy-done.13, s32[2,2,5,5,64]{4,3,2,1,0:T(8,128)S(1)} %copy-done.5, f32[2,2,5,5]{3,2,1,0:T(8,128)S(1)} %copy-done.12, s32[2,2,5,5,64]{4,3,2,1,0:T(8,128)S(1)} %copy-done.4, ...), kind=kOutput, calls=%fused_computation.226 | convolution fusion | flops 159334400 | bytes 7376000 | tf_op jit(solution)/shard_map/dtcariv,dtarjv->dtcarij/dot_general | solution.py:130
  92.3 1.4 slice.307
  93.7 5.2 %copy.181 = bf16[2,2,2,5,64,5,64]{6,5,4,3,2,1,0:T(8,128)(2,1)} copy(bf16[2,2,2,5,64,5,64]{4,6,2,5,3,1,0:T(8,128)(2,1)S(1)} %get-tuple-element.79) | data formatting | bytes 3276800 | tf_op jit(solution)/shard_map/convert_element_type | solution.py:132
  98.9 3.2 %copy.182 = bf16[1,2,2,5,64,5,64]{6,5,4,3,2,1,0:T(8,128)(2,1)S(1)} copy(bf16[1,2,2,5,64,5,64]{4,6,2,5,3,1,0:T(8,128)(2,1)} %slice.307) | data formatting | bytes 1638400 | tf_op jit(solution)/shard_map/slice | solution.py:158
  102.2 2.2 slice.274
  104.3 1.5 collective-permute-start.2
  105.8 7.2 %reshape.241 = bf16[2,2,2,320,320]{4,3,2,1,0:T(8,128)(2,1)} reshape(bf16[2,2,2,5,64,5,64]{6,5,4,3,2,1,0:T(8,128)(2,1)} %copy.181) | data formatting | bytes 3276800 | tf_op jit(solution)/shard_map/reshape | solution.py:133
  113.0 19.2 %all-reduce.3.cloned.1.call-done = (bf16[1,2,5,64,5,64]{5,4,3,2,1,0:T(8,128)(2,1)}, bf16[1,2,5,64,5,64]{5,4,3,2,1,0:T(8,128)(2,1)}) async-done(((bf16[1,2,5,64,5,64]{5,4,3,2,1,0:T(8,128)(2,1)}, bf16[1,2,5,64,5,64]{5,4,3,2,1,0:T(8,128)(2,1)}), (bf16[1,2,5,64,5,64]{5,4,3,2,1,0:T(8,128)(2,1)}, bf16[1,2,5,64,5,64]{5,4,3,2,1,0:T(8,128)(2,1)})) %all-reduce.3.cloned.1.call-update) | async-done | bytes 819216 | tf_op jit(solution)/shard_map/psum | solution.py:33
  132.2 2.7 %maximum_convert_fusion.1 = f32[2,2,5,64,5,64]{5,4,3,2,1,0:T(8,128)S(1)} fusion(bf16[1,2,5,64,5,64]{5,4,3,2,1,0:T(8,128)(2,1)} %get-tuple-element.18, bf16[1,2,5,64,5,64]{5,4,3,2,1,0:T(8,128)(2,1)} %get-tuple-element.19), kind=kLoop, calls=%fused_computation.30 | loop fusion | flops 819200 | bytes 2457600 | tf_op jit(solution)/shard_map/convert_element_type | solution.py:65
  135.5 2.0 slice_bitcast_fusion.3
  137.5 2.9 %copy.155 = f32[2,5,64,5,64]{2,4,3,1,0:T(8,128)} copy(f32[2,5,64,5,64]{4,3,2,1,0:T(8,128)} %get-tuple-element.24) | data formatting | bytes 1638400 | tf_op jit(solution)/shard_map/mul | solution.py:75
  140.4 1.7 copy.176
  142.0 5.0 %add_reduce_fusion.1 = (f32[2,2,5,5]{3,2,1,0:T(8,128)S(1)}, f32[2,2,5,5]{3,2,1,0:T(8,128)S(1)}, f32[2,2,5,5]{3,2,1,0:T(8,128)S(1)}) fusion(f32[2,2,2,5,64,5,64]{4,6,2,5,3,1,0:T(8,128)} %get-tuple-element.78, f32[2,5,64,5,64]{2,4,3,1,0:T(8,128)} %copy.176, f32[2,5,64,5,64]{2,4,3,1,0:T(8,128)} %copy.155), kind=kLoop, calls=%fused_computation.6 | loop fusion | flops 4914900 | bytes 4916400 | tf_op jit(solution)/shard_map/reduce_sum | solution.py:75
  147.1 1.8 maximum_convert_fusion
  148.9 2.8 %multiply_add_fusion.2 = (f32[2,2,1,320,320]{4,3,2,1,0:T(8,128)}, f32[2,2,1,320,320]{4,3,2,1,0:T(8,128)}, f32[2,2,1,320,320]{4,3,2,1,0:T(8,128)}, f32[2,2,1,320,320]{4,3,2,1,0:T(8,128)S(1)}) fusion(f32[3,2,2,320,320]{4,3,2,1,0:T(8,128)S(1)} %maximum_convert_fusion), kind=kLoop, calls=%fused_computation.35 | loop fusion | flops 4915200 | bytes 13107200 | tf_op jit(solution)/shard_map/add | solution.py:91
  151.7 9.1 %add.572 = f32[2,2,64,5,16,20]{5,4,3,2,1,0:T(8,128)} reshape(f32[2,2,1,320,320]{4,3,2,1,0:T(8,128)} %get-tuple-element.20) | data formatting | bytes 3276800 | tf_op jit(solution)/shard_map/add | solution.py:91
  160.8 9.0 %add.574 = f32[2,2,64,5,16,20]{5,4,3,2,1,0:T(8,128)} reshape(f32[2,2,1,320,320]{4,3,2,1,0:T(8,128)} %get-tuple-element.21) | data formatting | bytes 3276800 | tf_op jit(solution)/shard_map/add | solution.py:93
  169.8 4.8 %reduce_sum.102 = f32[2,2,64,16]{3,2,1,0:T(8,128)S(1)} reduce(f32[2,2,64,5,16,20]{5,4,3,2,1,0:T(8,128)} %add.572, f32[]{:T(128)} %constant.98.clone.1), dimensions={3,5}, to_apply=%region_8.10 | reduce | flops 405504 | bytes 1654788 | tf_op jit(solution)/shard_map/reduce_sum | solution.py:101
  174.6 4.8 %reduce_sum.103 = f32[2,2,64,16]{3,2,1,0:T(8,128)S(1)} reduce(f32[2,2,64,5,16,20]{5,4,3,2,1,0:T(8,128)} %add.574, f32[]{:T(128)} %constant.98.clone.1), dimensions={3,5}, to_apply=%region_9.11 | reduce | flops 405504 | bytes 1654788 | tf_op jit(solution)/shard_map/reduce_sum | solution.py:101
  179.4 9.1 %add.577 = f32[2,2,64,5,16,20]{5,4,3,2,1,0:T(8,128)} reshape(f32[2,2,1,320,320]{4,3,2,1,0:T(8,128)} %get-tuple-element.22) | data formatting | bytes 3276800 | tf_op jit(solution)/shard_map/add | solution.py:94
  188.5 4.8 %reduce_sum.104 = f32[2,2,64,16]{3,2,1,0:T(8,128)S(1)} reduce(f32[2,2,64,5,16,20]{5,4,3,2,1,0:T(8,128)} %add.577, f32[]{:T(128)} %constant.98.clone.1), dimensions={3,5}, to_apply=%region_10.12 | reduce | flops 405504 | bytes 1654788 | tf_op jit(solution)/shard_map/reduce_sum | solution.py:101
  193.3 7.9 %sub.65 = f32[2,2,64,5,16,20]{5,4,3,2,1,0:T(8,128)} reshape(f32[2,2,1,320,320]{4,3,2,1,0:T(8,128)S(1)} %get-tuple-element.23) | data formatting | bytes 3276800 | tf_op jit(solution)/shard_map/sub | solution.py:92
  201.2 4.8 %reduce_sum.105 = f32[2,2,64,16]{3,2,1,0:T(8,128)S(1)} reduce(f32[2,2,64,5,16,20]{5,4,3,2,1,0:T(8,128)} %sub.65, f32[]{:T(128)} %constant.98.clone.1), dimensions={3,5}, to_apply=%region_11.13 | reduce | flops 405504 | bytes 1654788 | tf_op jit(solution)/shard_map/reduce_sum | solution.py:101
  206.3 0.9 reshape.244
  207.3 3.5 %all-to-all-start = ((f32[16,1,512]{2,1,0:T(1,128)}), f32[16,1,512]{2,1,0:T(1,128)S(1)}, u32[]{:S(2)}, u32[]{:S(2)}) async-start(f32[16,1,512]{2,1,0:T(1,128)} %reshape.244), calls=%async_computation | async-start | bytes 65536 | tf_op jit(solution)/shard_map/all_to_all | solution.py:161
  211.4 6.0 %all-to-all-done = f32[16,1,512]{2,1,0:T(1,128)S(1)} async-done(((f32[16,1,512]{2,1,0:T(1,128)}), f32[16,1,512]{2,1,0:T(1,128)S(1)}, u32[]{:S(2)}, u32[]{:S(2)}) %all-to-all-start) | async-done | bytes 32800 | tf_op jit(solution)/shard_map/all_to_all | solution.py:161
  219.3 0.8 copy.186
  (98 shorter events, 21.4 us)
Async XLA Ops:
  7.2 125.0 %all-reduce.3.cloned.1.call-start = ((), (), s32[]{:S(2)}) async-start(), calls=%async_computation.1 | async-start | bytes 5242880 | tf_op jit(solution)/shard_map/psum | solution.py:33
  8.2 33.4 %collective-permute-start.1 = (bf16[2,2,2,344,12]{3,4,2,1,0:T(8,128)(2,1)S(1)}, bf16[2,2,2,344,12]{3,4,2,1,0:T(8,128)(2,1)S(1)}, u32[]{:S(2)}, u32[]{:S(2)}) collective-permute-start(bf16[2,2,2,344,12]{3,4,2,1,0:T(8,128)(2,1)S(1)} %get-tuple-element.28), channel_id=1, source_target_pairs={{1,0},{3,2},{5,4},{7,6},{9,8},{11,10},{13,12},{15,14},{17,16},{19,... | collective-permute-start | bytes 198152 | tf_op jit(solution)/shard_map/ppermute | solution.py:26
  9.5 29.1 %collective-permute-start = (bf16[2,2,2,344,12]{3,4,2,1,0:T(8,128)(2,1)S(1)}, bf16[2,2,2,344,12]{3,4,2,1,0:T(8,128)(2,1)S(1)}, u32[]{:S(2)}, u32[]{:S(2)}) collective-permute-start(bf16[2,2,2,344,12]{3,4,2,1,0:T(8,128)(2,1)S(1)} %get-tuple-element.29), channel_id=1, source_target_pairs={{0,1},{2,3},{4,5},{6,7},{8,9},{10,11},{12,13},{14,15},{16,17},{18,... | collective-permute-start | bytes 198152 | tf_op jit(solution)/shard_map/ppermute | solution.py:23
  23.6 3.2 %copy-start.7 = (s32[2,2,2,5,5]{4,2,3,1,0:T(2,128)S(1)}, s32[2,2,2,5,5]{4,2,3,1,0:T(2,128)}, u32[]{:S(2)}) copy-start(s32[2,2,2,5,5]{4,2,3,1,0:T(2,128)} %param.6) | copy-start | bytes 2404
  23.6 3.3 %copy-start.8 = (s32[2,2,2,5,5]{4,2,3,1,0:T(2,128)S(1)}, s32[2,2,2,5,5]{4,2,3,1,0:T(2,128)}, u32[]{:S(2)}) copy-start(s32[2,2,2,5,5]{4,2,3,1,0:T(2,128)} %param.7) | copy-start | bytes 2404
  25.2 8.9 %copy-start = (bf16[2,2,2,344,320]{3,4,2,1,0:T(8,128)(2,1)S(1)}, bf16[2,2,2,344,320]{3,4,2,1,0:T(8,128)(2,1)}, u32[]{:S(2)}) copy-start(bf16[2,2,2,344,320]{3,4,2,1,0:T(8,128)(2,1)} %param.5) | copy-start | bytes 5283844
  58.0 7.3 %copy-start.15 = (f32[2,2,5,5]{3,2,1,0:T(8,128)S(1)}, f32[2,2,5,5]{3,2,1,0:T(8,128)}, u32[]{:S(2)}) copy-start(f32[2,2,5,5]{3,2,1,0:T(8,128)} %copy.168) | copy-start | bytes 1204
  65.3 13.3 %copy-start.2 = (s32[2,2,5,5,64]{4,3,2,1,0:T(8,128)S(1)}, s32[2,2,5,5,64]{4,3,2,1,0:T(8,128)}, u32[]{:S(2)}) copy-start(s32[2,2,5,5,64]{4,3,2,1,0:T(8,128)} %get-tuple-element.93) | copy-start | bytes 76804
  65.3 13.3 %copy-start.3 = (s32[2,2,5,5,64]{4,3,2,1,0:T(8,128)S(1)}, s32[2,2,5,5,64]{4,3,2,1,0:T(8,128)}, u32[]{:S(2)}) copy-start(s32[2,2,5,5,64]{4,3,2,1,0:T(8,128)} %get-tuple-element.94) | copy-start | bytes 76804
  65.3 13.3 %copy-start.4 = (s32[2,2,5,5,64]{4,3,2,1,0:T(8,128)S(1)}, s32[2,2,5,5,64]{4,3,2,1,0:T(8,128)}, u32[]{:S(2)}) copy-start(s32[2,2,5,5,64]{4,3,2,1,0:T(8,128)} %get-tuple-element.95) | copy-start | bytes 76804
  65.3 13.3 %copy-start.5 = (s32[2,2,5,5,64]{4,3,2,1,0:T(8,128)S(1)}, s32[2,2,5,5,64]{4,3,2,1,0:T(8,128)}, u32[]{:S(2)}) copy-start(s32[2,2,5,5,64]{4,3,2,1,0:T(8,128)} %get-tuple-element.96) | copy-start | bytes 76804
  65.3 13.3 %copy-start.6 = (s32[2,2,5,5,64]{4,3,2,1,0:T(8,128)S(1)}, s32[2,2,5,5,64]{4,3,2,1,0:T(8,128)}, u32[]{:S(2)}) copy-start(s32[2,2,5,5,64]{4,3,2,1,0:T(8,128)} %get-tuple-element.97) | copy-start | bytes 76804
  65.3 13.3 %copy-start.9 = (f32[2,2,5,5]{3,2,1,0:T(8,128)S(1)}, f32[2,2,5,5]{3,2,1,0:T(8,128)}, u32[]{:S(2)}) copy-start(f32[2,2,5,5]{3,2,1,0:T(8,128)} %copy.160) | copy-start | bytes 1204
  65.3 13.3 %copy-start.10 = (f32[2,2,5,5]{3,2,1,0:T(8,128)S(1)}, f32[2,2,5,5]{3,2,1,0:T(8,128)}, u32[]{:S(2)}) copy-start(f32[2,2,5,5]{3,2,1,0:T(8,128)} %copy.161) | copy-start | bytes 1204
  65.3 13.3 %copy-start.11 = (f32[2,2,5,5]{3,2,1,0:T(8,128)S(1)}, f32[2,2,5,5]{3,2,1,0:T(8,128)}, u32[]{:S(2)}) copy-start(f32[2,2,5,5]{3,2,1,0:T(8,128)} %copy.162) | copy-start | bytes 1204
  65.3 13.3 %copy-start.12 = (f32[2,2,5,5]{3,2,1,0:T(8,128)S(1)}, f32[2,2,5,5]{3,2,1,0:T(8,128)}, u32[]{:S(2)}) copy-start(f32[2,2,5,5]{3,2,1,0:T(8,128)} %copy.163) | copy-start | bytes 1204
  65.3 13.3 %copy-start.13 = (f32[2,2,5,5]{3,2,1,0:T(8,128)S(1)}, f32[2,2,5,5]{3,2,1,0:T(8,128)}, u32[]{:S(2)}) copy-start(f32[2,2,5,5]{3,2,1,0:T(8,128)} %copy.164) | copy-start | bytes 1204
  65.3 13.3 %copy-start.14 = (f32[2,2,5,5]{3,2,1,0:T(8,128)S(1)}, f32[2,2,5,5]{3,2,1,0:T(8,128)}, u32[]{:S(2)}) copy-start(f32[2,2,5,5]{3,2,1,0:T(8,128)} %copy.157) | copy-start | bytes 1204
  104.3 42.8 %collective-permute-start.2 = (bf16[1,2,2,320,320]{4,3,2,1,0:T(8,128)(2,1)}, bf16[1,2,2,320,320]{4,3,2,1,0:T(8,128)(2,1)}, u32[]{:S(2)}, u32[]{:S(2)}) collective-permute-start(bf16[1,2,2,320,320]{4,3,2,1,0:T(8,128)(2,1)} %slice.274), channel_id=1, source_target_pairs={{2,0},{4,2},{6,4},{8,6},{10,8},{12,10},{14,12},{16,14},{18,16},{20... | collective-permute-start | bytes 2457608 | tf_op jit(solution)/shard_map/ppermute | solution.py:39
  142.0 5.1 %copy-start.1 = (bf16[2,2,2,320,320]{4,3,2,1,0:T(8,128)(2,1)S(1)}, bf16[2,2,2,320,320]{4,3,2,1,0:T(8,128)(2,1)}, u32[]{:S(2)}) copy-start(bf16[2,2,2,320,320]{4,3,2,1,0:T(8,128)(2,1)} %reshape.241) | copy-start | bytes 4915204
  207.3 10.1 %all-to-all-start = ((f32[16,1,512]{2,1,0:T(1,128)}), f32[16,1,512]{2,1,0:T(1,128)S(1)}, u32[]{:S(2)}, u32[]{:S(2)}) async-start(f32[16,1,512]{2,1,0:T(1,128)} %reshape.244), calls=%async_computation | async-start | bytes 65536 | tf_op jit(solution)/shard_map/all_to_all | solution.py:161
Sparse Core Ops, SparseCore 0:
  26.9 105.2 all-reduce.2
where the time goes:
time: 228 us; the launch traced here: 227 us
  local copies, waits for them, and re-layouts  98.4 us (43%)
  other arithmetic  45.7 us (20%)
  matrix products  26.8 us (12%)
  waiting for transfers between devices  25.2 us (11%)
  between operations  19.6 us (9%)
  starting transfers between devices  11.2 us (5%)
    psum x1, waiting for transfers between devices, spread(): return lax.psum(kept, axis)  19.2 us
    reduce_sum x4, other arithmetic, box_sum(): return jnp.sum(blocked, axis=(3, 5))  19.2 us
    unnamed x55, local copies, waits for them, and re-layouts  17.1 us
    dot_general x1, matrix products, resample(): jnp.einsum('dtcariv,dtarjv->dtcarij', partial_rows, across, preferred_ele...  13.6 us
    dot_general x1, matrix products, resample(): jnp.einsum('dtariw,dtcarwv->dtcariv', azimuth, windows, preferred_element...  13.2 us
    add x1, local copies, waits for them, and re-layouts, multilook_pairs(): power_later = later_real * later_real + later_imag * later_imag  9.09 us
    add x1, local copies, waits for them, and re-layouts, multilook_pairs(): cross_real = early_real * later_real + early_imag * later_imag  9.08 us
    add x1, local copies, waits for them, and re-layouts, multilook_pairs(): power_early = early_real * early_real + early_imag * early_imag  9.02 us
  transfers between devices with their start and end apart: 5, of which 2 were waited for; matrix products, arithmetic and copies ran while one was open for 47% of the time, Pallas kernels for 0%

commit v1 on v0

v1 whole, which is shorter than its diff:
```python
import functools

import jax
import jax.numpy as jnp
from jax import lax
from jax.experimental import pallas as pl
from jax.experimental.pallas import tpu as pltpu
from jax.sharding import PartitionSpec as P

TILE_COUNT = 2
CHIP_SIZE = 64
TAP_COUNT = 8
SUBSTEPS = 64
LOOK_AZ = 5
LOOK_RG = 20
MARGIN = 12
LANES = 128
GROUP = 8

epsilon = 1e-06
MESH = pl.DeviceIdType.MESH


def halo(block, width, dim):
    count = lax.axis_size("strip")
    forward = [(i, i + 1) for i in range(count - 1)]
    backward = [(target, source) for source, target in forward]
    low = lax.ppermute(
        lax.slice_in_dim(block, block.shape[dim] - width, None, axis=dim), "strip", forward
    )
    high = lax.ppermute(lax.slice_in_dim(block, 0, width, axis=dim), "strip", backward)
    return low, high


def tap_weights(fraction_part):
    offset = fraction_part.astype(jnp.float32) / SUBSTEPS
    tap_axis = jnp.arange(TAP_COUNT).astype(jnp.float32)
    distance = tap_axis - (TAP_COUNT // 2 - 1) - offset[..., None]
    weights = jnp.sinc(distance) * (0.5 + 0.5 * jnp.cos(jnp.pi * distance / (TAP_COUNT // 2)))
    return weights / jnp.sum(weights, axis=-1, keepdims=True)


def tap_vectors(shifts, fractions):
    weights = tap_weights(fractions)
    first = shifts + (MARGIN - TAP_COUNT // 2 + 1)
    base = (jnp.arange(shifts.shape[-1], dtype=jnp.int32) % 2) * CHIP_SIZE
    lane = jnp.arange(LANES, dtype=jnp.int32)
    lines = jnp.zeros(shifts.shape[1:] + (LANES,), jnp.float32)
    columns = lines
    for k in range(TAP_COUNT):
        lines = lines + jnp.where(
            lane == (first[0] + k)[..., None], weights[0, ..., k][..., None], 0.0
        )
        columns = columns + jnp.where(
            lane == ((base - first[1] - k) % LANES)[..., None],
            weights[1, ..., k][..., None],
            0.0,
        )
    return lines, columns


def spread_rows(row, count):
    tall = jnp.broadcast_to(row, (count, LANES))
    return pltpu.roll(tall, 0, 1, stride=1, stride_axis=0)


def split_dot(values, selector):
    high = values.astype(jnp.bfloat16)
    low = (values - high.astype(jnp.float32)).astype(jnp.bfloat16)
    return jnp.dot(high, selector, preferred_element_type=jnp.float32) + jnp.dot(
        low, selector, preferred_element_type=jnp.float32
    )


def kernel(
    n, dims,
    even_ref, odd_ref, lines_ref, cols_ref, cand_ref,
    coh_ref, sums_ref,
    series, sent, got, acc, part_buf, whole, looks, chip_rows, out_buf,
    ref_send, ref_recv, next_send, next_recv, coh_send, coh_recv,
):
    tiles, chips_az, chips_rg, rows, cols = dims
    me = lax.axis_index("date")
    bits = n.bit_length() - 1
    groups = cand_ref.shape[0]
    blocks = series.shape[3]
    wide = blocks * LANES
    bf16 = jnp.bfloat16
    f32 = jnp.float32

    barrier = pltpu.get_barrier_semaphore()
    for o in range(1, n):
        pl.semaphore_signal(
            barrier, inc=1, device_id={"date": lax.rem(me + o, n)}, device_id_type=MESH
        )
    pl.semaphore_wait(barrier, n - 1)

    offsets = [jnp.int32(0)]
    for b in range(bits):
        offsets.append(offsets[-1] + ((me // (1 << b)) % 2) * (groups >> (b + 1)))

    def partner(b):
        return me + (1 - 2 * ((me // (1 << b)) % 2)) * (1 << b)

    def halving(b):
        half = groups >> (b + 1)
        away = offsets[b] + (1 - (me // (1 << b)) % 2) * half
        source = cand_ref if b == 0 else acc
        return pltpu.make_async_remote_copy(
            src_ref=source.at[pl.ds(away, half)],
            dst_ref=part_buf.at[pl.ds(groups - 2 * half, half)],
            send_sem=ref_send.at[b],
            recv_sem=ref_recv.at[b],
            device_id={"date": partner(b)},
            device_id_type=MESH,
        )

    def add_half(b):
        half = groups >> (b + 1)
        source = cand_ref if b == 0 else acc
        target = whole if b == bits - 1 else acc

        def body(i, carry):
            g = offsets[b + 1] + i
            target[g] = source[g] + part_buf[groups - 2 * half + i]
            return carry

        lax.fori_loop(0, half, body, 0)

    def doubling(b):
        half = groups >> (b + 1)
        mine = whole.at[pl.ds(offsets[b + 1], half)]
        return pltpu.make_async_remote_copy(
            src_ref=mine,
            dst_ref=mine,
            send_sem=ref_send.at[bits + b],
            recv_sem=ref_recv.at[bits + b],
            device_id={"date": partner(b)},
            device_id_type=MESH,
        )

    state = {"step": 0, "copy": None}

    def advance():
        step = state["step"]
        if step > 2 * bits:
            return
        if step > 0:
            state["copy"].wait()
            if step <= bits:
                add_half(step - 1)
        if step < bits:
            state["copy"] = halving(step)
            state["copy"].start()
        elif step < 2 * bits:
            state["copy"] = doubling(2 * bits - 1 - step)
            state["copy"].start()
        state["step"] = step + 1

    lane = lax.broadcasted_iota(jnp.int32, (LANES, LANES), 1)
    window = 96

    def resample(d, t, first, last):
        def chip_line(a, carry):
            row0 = pl.multiple_of(a * CHIP_SIZE, CHIP_SIZE)
            q = (d * tiles + t) * 2
            for m in range((chips_rg + 1) // 2):
                span = slice(m * LANES, (m + 1) * LANES)
                halves = []
                mats = []
                for side, src in ((0, even_ref), (1, odd_ref)):
                    r = 2 * m + side
                    if r >= chips_rg:
                        continue
                    line_row = lines_ref[d * tiles + t, a, r : r + 1, :]
                    col_row = cols_ref[d * tiles + t, a, r : r + 1, :]
                    line_mat = spread_rows(line_row, CHIP_SIZE).astype(bf16)[:, :window]
                    col_mat = spread_rows(col_row, LANES)
                    keep = lane < CHIP_SIZE if side == 0 else lane >= CHIP_SIZE
                    mats.append(jnp.where(keep, col_mat, 0.0).astype(bf16))
                    both = jnp.concatenate(
                        [src[q, pl.ds(row0, window), span], src[q + 1, pl.ds(row0, window), span]],
                        axis=1,
                    )
                    halves.append(
                        jnp.dot(line_mat, both, preferred_element_type=f32).astype(bf16)
                    )
                re = jnp.concatenate([h[:, :LANES] for h in halves], axis=1)
                im = jnp.concatenate([h[:, LANES:] for h in halves], axis=1)
                stacked = jnp.concatenate([re, im], axis=0)
                matrix = jnp.concatenate(mats, axis=0)
                out = jnp.dot(stacked, matrix, preferred_element_type=f32).astype(bf16)
                for c in range(2):
                    piece = out[c * CHIP_SIZE : (c + 1) * CHIP_SIZE]
                    series[d, t, c, m, pl.ds(row0, CHIP_SIZE), :] = piece.astype(f32)
                    if d == 0:
                        sent[t, c, m, pl.ds(row0, CHIP_SIZE), :] = piece
            return carry

        lax.fori_loop(first, last, chip_line, 0)

    advance()
    middle = (chips_az + 1) // 2
    last_d = series.shape[0] - 2
    following = [None]
    for d in range(last_d + 1):
        for t in range(tiles):
            resample(d, t, 0, middle)
            advance()
            resample(d, t, middle, chips_az)
            if d == 0 and t == tiles - 1:
                following[0] = pltpu.make_async_remote_copy(
                    src_ref=sent, dst_ref=got, send_sem=next_send, recv_sem=next_recv,
                    device_id={"date": lax.rem(me + n - 1, n)}, device_id_type=MESH,
                )

                @pl.when(me > 0)
                def _():
                    following[0].start()

    @pl.when(me < n - 1)
    def _():
        following[0].wait_recv()

        def body(i, carry):
            row = pl.multiple_of(i * 16, 16)
            for t in range(tiles):
                for c in range(2):
                    for m in range(blocks):
                        series[last_d + 1, t, c, m, pl.ds(row, 16), :] = got[
                            t, c, m, pl.ds(row, 16), :
                        ].astype(f32)
            return carry

        lax.fori_loop(0, rows // 16, body, 0)

    @pl.when(me == n - 1)
    def _():
        series[last_d + 1] = jnp.zeros(series.shape[1:], f32)

    advance()
    dates = series.shape[0]
    pairs = dates - 1
    look_rows = rows // LOOK_AZ
    for t in range(tiles):
        def look_block(y, carry):
            def add(total, value):
                return value if total is None else total + value

            row = pl.multiple_of(y * GROUP, GROUP)
            for m in range(blocks):
                span = slice(m * LANES, (m + 1) * LANES)
                power = [None] * dates
                cross = [[None, None] for _ in range(pairs)]
                for s in range(LOOK_AZ):
                    lines_at = pl.ds(y * (GROUP * LOOK_AZ) + s, GROUP, stride=LOOK_AZ)
                    here = [
                        [series[d, t, c, m, lines_at, :] for c in range(2)] for d in range(dates)
                    ]
                    for d in range(dates):
                        re, im = here[d]
                        power[d] = add(power[d], re * re + im * im)
                    for p in range(pairs):
                        ar, ai = here[p]
                        br, bi = here[p + 1]
                        cross[p][0] = add(cross[p][0], ar * br + ai * bi)
                        cross[p][1] = add(cross[p][1], ai * br - ar * bi)
                for d in range(dates):
                    looks[t, d, pl.ds(row, GROUP), span] = power[d]
                for p in range(pairs):
                    for c in range(2):
                        looks[t, dates + 2 * p + c, pl.ds(row, GROUP), span] = cross[p][c]
            return carry

        lax.fori_loop(0, look_rows // GROUP, look_block, 0)
        advance()

    looks_rg = cols // LOOK_RG
    col_id = lax.broadcasted_iota(jnp.int32, (wide, LANES), 0)
    lane_id = lax.broadcasted_iota(jnp.int32, (wide, LANES), 1)
    base = col_id - LOOK_RG * lane_id

    def selector(q):
        shifted = base + LOOK_RG * looks_rg * q
        hit = (shifted >= 0) & (shifted < LOOK_RG) & (col_id < cols)
        return jnp.where(hit, 1.0, 0.0).astype(f32)

    numer = jnp.zeros((look_rows, LANES), f32)
    early = jnp.zeros((look_rows, LANES), f32)
    later = jnp.zeros((look_rows, LANES), f32)
    for p in range(pairs):
        for t in range(tiles):
            picks = [selector((c * pairs + p) * tiles + t) for c in range(2)]
            for c in range(2):
                numer = numer + split_dot(looks[t, dates + 2 * p + c], picks[c].astype(bf16))
            pick = (picks[0] + picks[1]).astype(bf16)
            early = early + split_dot(looks[t, p], pick)
            later = later + split_dot(looks[t, p + 1], pick)
    coherence = numer / jnp.sqrt((early + epsilon) * (later + epsilon))
    share = look_rows // n
    for j in range(n):
        out_buf[j] = coherence[j * share : (j + 1) * share]
    coh_ref[me] = out_buf[me]
    copies = []
    for o in range(1, n):
        peer = lax.rem(me + o, n)
        copy = pltpu.make_async_remote_copy(
            src_ref=out_buf.at[peer], dst_ref=coh_ref.at[me],
            send_sem=coh_send.at[o], recv_sem=coh_recv.at[o],
            device_id={"date": peer}, device_id_type=MESH,
        )
        copy.start()
        copies.append(copy)
    while state["step"] <= 2 * bits:
        advance()

    line_groups = CHIP_SIZE // GROUP
    kept = dates - 1
    for t in range(tiles):
        def corr_line(a, carry):
            for m in range(blocks):
                low = m * LANES
                size = min(LANES, cols - low)
                span = slice(low, low + size)
                total = [jnp.zeros((GROUP, size), f32)] * (1 + 3 * kept)
                for g in range(line_groups):
                    at = a * line_groups + g
                    rr = whole[(t * 2) * (rows // GROUP) + at, :, span].astype(f32)
                    ri = whole[(t * 2 + 1) * (rows // GROUP) + at, :, span].astype(f32)
                    total[0] = total[0] + (rr * rr + ri * ri)
                    row = pl.multiple_of(at * GROUP, GROUP)
                    for d in range(kept):
                        sr = series[d, t, 0, m, pl.ds(row, GROUP), :size]
                        si = series[d, t, 1, m, pl.ds(row, GROUP), :size]
                        total[1 + 3 * d] = total[1 + 3 * d] + (rr * sr + ri * si)
                        total[2 + 3 * d] = total[2 + 3 * d] + (ri * sr - rr * si)
                        total[3 + 3 * d] = total[3 + 3 * d] + (sr * sr + si * si)
                for k in range(1 + 3 * kept):
                    chip_rows[t, a, k : k + 1, span] = jnp.sum(total[k], axis=0, keepdims=True)
            return carry

        lax.fori_loop(0, chips_az, corr_line, 0)
    col_id = lax.broadcasted_iota(jnp.int32, (cols, LANES), 0)
    lane_id = lax.broadcasted_iota(jnp.int32, (cols, LANES), 1)
    gap = col_id - CHIP_SIZE * lane_id
    pick = jnp.where((gap >= 0) & (gap < CHIP_SIZE), 1.0, 0.0).astype(bf16)
    for t in range(tiles):
        for a in range(chips_az):
            sums_ref[t, a] = split_dot(chip_rows[t, a], pick)

    for o in range(1, n):
        copies[o - 1].wait()

    @pl.when(me > 0)
    def _():
        following[0].wait_send()


def per_device(n, acquisitions, shifts, fractions, ref_dates):
    dates_local, tiles, _, all_rows, cols = acquisitions.shape
    rows = all_rows - 2 * MARGIN
    chips_az, chips_rg = shifts.shape[3:]
    wide = -(-cols // LANES) * LANES
    low, high = halo(acquisitions, MARGIN, 4)
    owners = ref_dates // dates_local
    slots = ref_dates % dates_local
    me = lax.axis_index("date")
    cand = jnp.stack(
        [
            jnp.where(
                owners[t] == me,
                lax.dynamic_index_in_dim(acquisitions[:, t], slots[t], 0, keepdims=False)[
                    :, MARGIN : MARGIN + rows, :
                ],
                0,
            ).astype(acquisitions.dtype)
            for t in range(tiles)
        ]
    ).reshape(tiles * 2 * rows // GROUP, GROUP, cols)
    padded = jnp.concatenate([low, acquisitions, high], axis=4)
    flat = padded.reshape((-1,) + padded.shape[3:])
    tall = -(-all_rows // 32) * 32
    even = jnp.pad(flat, ((0, 0), (0, tall - all_rows), (0, wide - flat.shape[2])))
    odd_wide = (chips_rg // 2) * LANES
    odd = even[:, :, CHIP_SIZE : CHIP_SIZE + odd_wide]
    lines, columns = tap_vectors(shifts, fractions)
    lines = lines.reshape((-1,) + lines.shape[2:])
    columns = columns.reshape((-1,) + columns.shape[2:])

    look_rows = rows // LOOK_AZ
    looks_rg = cols // LOOK_RG
    share = look_rows // n
    stat_rows = 1 + 3 * dates_local
    bits = n.bit_length() - 1
    vmem = pl.BlockSpec(memory_space=pltpu.VMEM)
    f32 = jnp.float32
    bf16 = jnp.bfloat16
    groups = cand.shape[0]
    dma = pltpu.SemaphoreType.DMA
    coh, sums = pl.pallas_call(
        functools.partial(kernel, n, (tiles, chips_az, chips_rg, rows, cols)),
        out_shape=(
            jax.ShapeDtypeStruct((n, share, LANES), f32),
            jax.ShapeDtypeStruct((tiles, chips_az, stat_rows, LANES), f32),
        ),
        in_specs=[vmem] * 5,
        out_specs=(vmem, vmem),
        scratch_shapes=[
            pltpu.VMEM((dates_local + 1, tiles, 2, wide // LANES, rows, LANES), f32),
            pltpu.VMEM((tiles, 2, wide // LANES, rows, LANES), bf16),
            pltpu.VMEM((tiles, 2, wide // LANES, rows, LANES), bf16),
            pltpu.VMEM((groups, GROUP, cols), bf16),
            pltpu.VMEM((groups, GROUP, cols), bf16),
            pltpu.VMEM((groups, GROUP, cols), bf16),
            pltpu.VMEM((tiles, dates_local + 1 + 2 * dates_local, look_rows, wide), f32),
            pltpu.VMEM((tiles, chips_az, stat_rows, cols), f32),
            pltpu.VMEM((n, share, LANES), f32),
            dma((2 * bits,)), dma((2 * bits,)), dma, dma, dma((n,)), dma((n,)),
        ],
        compiler_params=pltpu.CompilerParams(
            collective_id=0, has_side_effects=True, vmem_limit_bytes=50 * 1024 * 1024
        ),
    )(even, odd, lines, columns, cand)

    stats = sums[..., :chips_rg]
    ref_power = stats[:, :, 0]
    sec = stats[:, :, 1:].reshape(tiles, chips_az, dates_local, 3, chips_rg)
    sec = sec.transpose(3, 2, 0, 1, 4)
    denominator = jnp.sqrt((ref_power[None] + epsilon) * (sec[2] + epsilon))
    chip_corr = sec[:2] / denominator[None]
    looked = coh.reshape(n, share, 2, dates_local, tiles, looks_rg)
    looked = looked.transpose(2, 0, 3, 4, 1, 5).reshape(2, n * dates_local, tiles, share, looks_rg)
    return (chip_corr, looked[:, : n * dates_local - 1])


def solution(mesh):
    return jax.shard_map(
        functools.partial(per_device, mesh.shape["date"]),
        mesh=mesh,
        in_specs=(
            P("date", None, None, None, "strip"),
            P(None, "date", None, None, "strip"),
            P(None, "date", None, None, "strip"),
            P(),
        ),
        out_specs=(P(None, "date", None, None, "strip"), P(None, None, None, "date", "strip")),
        check_vma=False,
    )
```

time: 228 us -> 97.5 us (0.43)
  local copies, waits for them, and re-layouts: 98.4 us -> 21.7 us
  Pallas kernels: 0 us -> 50.9 us
  other arithmetic: 45.7 us -> 12.2 us
  matrix products: 26.8 us -> 0 us
  waiting for transfers between devices: 25.2 us -> 0.01 us
  between operations: 19.6 us -> 6.17 us
  starting transfers between devices: 11.2 us -> 6.17 us
    pallas_call x0 -> x1, Pallas kernels: none -> 50.9 us  [per_device(): pl.pallas_call(functools.partial(kernel, n, (tiles, chips_az, chips_rg, r...]
    dot_general x2 -> x0, matrix products: 26.8 us -> none  [the longest x1 13.6 us: resample(): jnp.einsum('dtcariv,dtarjv->dtcarij', partial_rows, across, preferred_ele...]
    reduce_sum x7 -> x1, other arithmetic: 28 us -> 3.21 us  [tap_weights(): return weights / jnp.sum(weights, axis=-1, keepdims=True)]
    add x7 -> x8, local copies, waits for them, and re-layouts: 27.2 us -> 4.22 us  [the longest x7 4.21 us: tap_vectors(): first[0] + k]
    psum x1 -> x0, waiting for transfers between devices: 19.2 us -> none  [spread(): return lax.psum(kept, axis)]
    unnamed x55 -> x36, local copies, waits for them, and re-layouts: 17.1 us -> 1.51 us
    another operation x5 -> x1, local copies, waits for them, and re-layouts: 11.3 us -> 1.61 us  [per_device(): jnp.stack([jnp.where(owners[t] == me, lax.dynamic_index_in_dim(acquisitio...]
    sub x1 -> x0, local copies, waits for them, and re-layouts: 7.93 us -> none  [multilook_pairs(): cross_imag = early_imag * later_real - early_real * later_imag]
  transfers between devices with their start and end apart: 5 -> 2, of which waited for: 2 -> 0; matrix products, arithmetic and copies ran while one was open for 47% -> 24% of each run, Pallas kernels for 0% -> 0%
where the time goes in v1:
time: 97.5 us; the launch traced here: 97.1 us
  Pallas kernels  50.9 us (52%)
  local copies, waits for them, and re-layouts  21.7 us (22%)
  other arithmetic  12.2 us (13%)
  starting transfers between devices  6.17 us (6%)
  between operations  6.17 us (6%)
    pallas_call x1, Pallas kernels, per_device(): pl.pallas_call(functools.partial(kernel, n, (tiles, chips_az, chips_rg, r...  50.9 us
    ppermute x1, starting transfers between devices, halo(): lax.ppermute(lax.slice_in_dim(block, block.shape[dim] - width, None, axis...  4.88 us
    broadcast_in_dim x8, local copies, waits for them, and re-layouts, tap_vectors(): jnp.where(lane == (first[0] + k)[..., None], weights[0, ..., k][..., None...  4.81 us
    add x7, local copies, waits for them, and re-layouts, tap_vectors(): first[0] + k  4.21 us
    reduce_sum x1, other arithmetic, tap_weights(): return weights / jnp.sum(weights, axis=-1, keepdims=True)  3.21 us
    div x1, other arithmetic, tap_weights(): return weights / jnp.sum(weights, axis=-1, keepdims=True)  3.13 us
    concatenate x1, local copies, waits for them, and re-layouts, per_device(): padded = jnp.concatenate([low, acquisitions, high], axis=4)  3 us
  transfers between devices with their start and end apart: 2, of which 0 were waited for; matrix products, arithmetic and copies ran while one was open for 24% of the time, Pallas kernels for 0%

profile of v1, /device:TPU:0, one launch (start us, length us, event | category | flops | bytes accessed | tf_op | source)
XLA Modules:
  0.0 97.1 jit_solution(11200304028847035128)
XLA Ops:
  0.6 1.0 %fusion.28 = (bf16[2,2,2,344,12]{3,4,2,1,0:T(8,128)(2,1)S(1)}, bf16[2,2,2,344,12]{3,4,2,1,0:T(8,128)(2,1)S(1)}) fusion(bf16[2,2,2,344,320]{3,4,2,1,0:T(8,128)(2,1)} %param.4), kind=kLoop, calls=%fused_computation.111 | loop fusion | bytes 264192 | tf_op jit(solution)/shard_map/slice | solution.py:29
  1.6 4.9 %collective-permute-start = (bf16[2,2,2,344,12]{3,4,2,1,0:T(8,128)(2,1)S(1)}, bf16[2,2,2,344,12]{3,4,2,1,0:T(8,128)(2,1)S(1)}, u32[]{:S(2)}, u32[]{:S(2)}) collective-permute-start(bf16[2,2,2,344,12]{3,4,2,1,0:T(8,128)(2,1)S(1)} %get-tuple-element.12), channel_id=1, source_target_pairs={{0,1},{2,3},{4,5},{6,7},{8,9},{10,11},{12,13},{14,15},{16,17},{18,... | collective-permute-start | bytes 198152 | tf_op jit(solution)/shard_map/ppermute | solution.py:28
  6.5 1.3 %collective-permute-start.1 = (bf16[2,2,2,344,12]{3,4,2,1,0:T(8,128)(2,1)S(1)}, bf16[2,2,2,344,12]{3,4,2,1,0:T(8,128)(2,1)S(1)}, u32[]{:S(2)}, u32[]{:S(2)}) collective-permute-start(bf16[2,2,2,344,12]{3,4,2,1,0:T(8,128)(2,1)S(1)} %get-tuple-element.13), channel_id=1, source_target_pairs={{1,0},{3,2},{5,4},{7,6},{9,8},{11,10},{13,12},{15,14},{17,16},{19,... | collective-permute-start | bytes 198152 | tf_op jit(solution)/shard_map/ppermute | solution.py:31
  7.8 0.7 and_select_fusion.1
  8.5 0.6 fusion.31
  11.5 0.7 broadcast_add_fusion
  12.3 0.0 copy-start.1
  12.3 1.7 %fusion.27 = (bf16[2,1,2,344,320]{3,4,2,1,0:T(8,128)(2,1)S(1)}, bf16[2,1,2,344,320]{3,4,2,1,0:T(8,128)(2,1)S(1)}) fusion(bf16[2,2,2,344,320]{3,4,2,1,0:T(8,128)(2,1)} %param.4), kind=kLoop, calls=%fused_computation.110 | loop fusion | bytes 3522560 | tf_op jit(solution)/shard_map/slice | solution.py:372
  15.3 0.6 copy.94
  15.9 0.6 copy.106
  16.5 0.6 copy.104
  17.1 0.6 copy.102
  17.7 0.6 copy.100
  18.3 0.6 copy.98
  18.9 0.6 copy.96
  19.5 0.1 add_select_fusion.7
  19.7 3.2 %fusion.14 = f32[2,2,2,5,5]{4,2,1,3,0:T(2,128)S(1)} fusion(f32[8]{0:T(128)S(1)} %convert_add_fusion, s32[2,2,2,5,5]{4,2,3,1,0:T(2,128)S(1)} %copy-done.1), kind=kLoop, calls=%fused_computation.51 | loop fusion | flops 62600 | bytes 1632 | tf_op jit(solution)/shard_map/reduce_sum | solution.py:40
  22.9 3.1 %broadcast_divide_fusion = f32[2,2,2,5,5,8]{4,2,1,3,5,0:T(2,128)S(1)} fusion(f32[2,2,2,5,5]{4,2,1,3,0:T(2,128)S(1)} %fusion.14, f32[8]{0:T(128)S(1)} %convert_add_fusion, s32[2,2,2,5,5]{4,2,3,1,0:T(2,128)S(1)} %copy-done.1), kind=kLoop, calls=%fused_computation.49 | loop fusion | flops 62800 | bytes 8032 | tf_op jit(solution)/shard_map/div | solution.py:40
  26.2 0.6 copy.107
  26.8 0.6 copy.105
  27.4 0.6 copy.103
  28.0 0.6 copy.101
  28.6 0.6 copy.99
  29.2 0.6 copy.97
  29.8 0.6 copy.95
  30.4 0.6 copy.93
  32.2 0.0 copy-start.3
  32.2 0.0 copy-start.9
  32.3 0.1 dynamic-slice_bitcast_fusion.1
  32.4 0.2 fusion.1
  32.6 0.1 dynamic-slice_bitcast_fusion
  32.7 0.2 fusion
  32.9 0.4 select_add_fusion.cols_ref
  33.4 0.0 copy-start
  33.5 0.4 select_add_fusion.1.lines_ref
  33.9 1.2 %pad_maximum_fusion.1 = bf16[2,2,320,320]{2,3,1,0:T(8,128)(2,1)} fusion(bf16[1,2,320,320]{2,3,1,0:T(8,128)(2,1)S(1)} %fusion, bf16[1,2,320,320]{2,3,1,0:T(8,128)(2,1)S(1)} %fusion.1), kind=kLoop, calls=%fused_computation.1 | loop fusion | flops 409600 | bytes 1638400 | tf_op jit(solution)/shard_map/stack | solution.py:368
  35.0 1.6 %copy.125 = bf16[2,2,320,320]{3,2,1,0:T(8,128)(2,1)S(1)} copy(bf16[2,2,320,320]{2,3,1,0:T(8,128)(2,1)} %pad_maximum_fusion.1) | data formatting | bytes 1638400 | tf_op jit(solution)/shard_map/stack | solution.py:368
  36.6 0.0 collective-permute-done
  36.7 0.0 collective-permute-done.1
  36.7 1.9 %pad_maximum_fusion = bf16[2,2,2,344,344]{3,4,2,1,0:T(8,128)(2,1)} fusion(bf16[2,2,2,344,12]{3,4,2,1,0:T(8,128)(2,1)S(1)} %collective-permute-done.1, bf16[2,2,2,344,320]{3,4,2,1,0:T(8,128)(2,1)S(1)} %copy-done, bf16[2,2,2,344,12]{3,4,2,1,0:T(8,128)(2,1)S(1)} %collective-permute-done), kind=kLoop, calls=%fused_computation | loop fusion | flops 5680128 | bytes 3786752 | tf_op jit(solution)/shard_map/concatenate | solution.py:380
  38.6 3.0 %copy.89 = bf16[2,2,2,344,344]{4,3,2,1,0:T(8,128)(2,1)S(1)} copy(bf16[2,2,2,344,344]{3,4,2,1,0:T(8,128)(2,1)} %pad_maximum_fusion) | data formatting | bytes 3786752 | tf_op jit(solution)/shard_map/concatenate | solution.py:380
  41.6 0.9 pad_slice_fusion.odd_ref
  42.5 1.6 %pad.4.even_ref = bf16[8,352,384]{2,1,0:T(8,128)(2,1)} pad(bf16[8,344,344]{2,1,0:T(8,128)(2,1)S(1)} %bitcast.46, bf16[]{:T(256)} %constant.148.clone.1), padding=0_0x0_8x0_40 | pad | bytes 4056066 | tf_op jit(solution)/shard_map/jit(_pad)/pad | solution.py:383
  44.1 50.9 %shard_map.59 = (f32[16,4,128]{2,1,0:T(4,128)S(1)}, f32[2,5,7,128]{3,2,1,0:T(8,128)S(1)}) custom-call(bf16[8,352,384]{2,1,0:T(8,128)(2,1)} %pad.4.even_ref, bf16[8,352,256]{2,1,0:T(8,128)(2,1)S(1)} %pad_slice_fusion.odd_ref, f32[4,5,5,128]{3,2,1,0:T(8,128)S(1)} %select_add_fusion.1.lines_ref, f32[4,5,5,128]{3,2,1,0:T(8,128)S(1)} %select_add_fusion.cols_ref, ...), custom_call_target="tpu_custom_call" | custom-call | tf_op jit(solution)/shard_map/pallas_call | solution.py:400
  95.1 0.6 copy.132
  95.7 0.4 reshape.291
  96.1 0.1 copy.131
  96.3 0.8 copy.133
  (60 shorter events, 0.3 us)
Async XLA Ops:
  1.6 35.0 %collective-permute-start = (bf16[2,2,2,344,12]{3,4,2,1,0:T(8,128)(2,1)S(1)}, bf16[2,2,2,344,12]{3,4,2,1,0:T(8,128)(2,1)S(1)}, u32[]{:S(2)}, u32[]{:S(2)}) collective-permute-start(bf16[2,2,2,344,12]{3,4,2,1,0:T(8,128)(2,1)S(1)} %get-tuple-element.12), channel_id=1, source_target_pairs={{0,1},{2,3},{4,5},{6,7},{8,9},{10,11},{12,13},{14,15},{16,17},{18,... | collective-permute-start | bytes 198152 | tf_op jit(solution)/shard_map/ppermute | solution.py:28
  6.5 30.2 %collective-permute-start.1 = (bf16[2,2,2,344,12]{3,4,2,1,0:T(8,128)(2,1)S(1)}, bf16[2,2,2,344,12]{3,4,2,1,0:T(8,128)(2,1)S(1)}, u32[]{:S(2)}, u32[]{:S(2)}) collective-permute-start(bf16[2,2,2,344,12]{3,4,2,1,0:T(8,128)(2,1)S(1)} %get-tuple-element.13), channel_id=1, source_target_pairs={{1,0},{3,2},{5,4},{7,6},{9,8},{11,10},{13,12},{15,14},{17,16},{19,... | collective-permute-start | bytes 198152 | tf_op jit(solution)/shard_map/ppermute | solution.py:31
  12.3 7.4 %copy-start.1 = (s32[2,2,2,5,5]{4,2,3,1,0:T(2,128)S(1)}, s32[2,2,2,5,5]{4,2,3,1,0:T(2,128)}, u32[]{:S(2)}) copy-start(s32[2,2,2,5,5]{4,2,3,1,0:T(2,128)} %param.6) | copy-start | bytes 2404
  32.2 1.1 %copy-start.2 = (s32[4,5,5]{2,1,0:T(8,128)S(1)}, s32[4,5,5]{2,1,0:T(8,128)}, u32[]{:S(2)}) copy-start(s32[4,5,5]{2,1,0:T(8,128)} %copy.94) | copy-start | bytes 1204
  32.2 1.1 %copy-start.3 = (s32[4,5,5]{2,1,0:T(8,128)S(1)}, s32[4,5,5]{2,1,0:T(8,128)}, u32[]{:S(2)}) copy-start(s32[4,5,5]{2,1,0:T(8,128)} %copy.106) | copy-start | bytes 1204
  32.2 1.1 %copy-start.4 = (s32[4,5,5]{2,1,0:T(8,128)S(1)}, s32[4,5,5]{2,1,0:T(8,128)}, u32[]{:S(2)}) copy-start(s32[4,5,5]{2,1,0:T(8,128)} %copy.104) | copy-start | bytes 1204
  32.2 1.1 %copy-start.5 = (s32[4,5,5]{2,1,0:T(8,128)S(1)}, s32[4,5,5]{2,1,0:T(8,128)}, u32[]{:S(2)}) copy-start(s32[4,5,5]{2,1,0:T(8,128)} %copy.102) | copy-start | bytes 1204
  32.2 1.1 %copy-start.6 = (s32[4,5,5]{2,1,0:T(8,128)S(1)}, s32[4,5,5]{2,1,0:T(8,128)}, u32[]{:S(2)}) copy-start(s32[4,5,5]{2,1,0:T(8,128)} %copy.100) | copy-start | bytes 1204
  32.2 1.1 %copy-start.7 = (s32[4,5,5]{2,1,0:T(8,128)S(1)}, s32[4,5,5]{2,1,0:T(8,128)}, u32[]{:S(2)}) copy-start(s32[4,5,5]{2,1,0:T(8,128)} %copy.98) | copy-start | bytes 1204
  32.2 1.1 %copy-start.8 = (s32[4,5,5]{2,1,0:T(8,128)S(1)}, s32[4,5,5]{2,1,0:T(8,128)}, u32[]{:S(2)}) copy-start(s32[4,5,5]{2,1,0:T(8,128)} %copy.96) | copy-start | bytes 1204
  32.2 1.1 %copy-start.9 = (f32[4,5,5]{2,1,0:T(8,128)S(1)}, f32[4,5,5]{2,1,0:T(8,128)}, u32[]{:S(2)}) copy-start(f32[4,5,5]{2,1,0:T(8,128)} %copy.107) | copy-start | bytes 1204
  32.3 1.1 %copy-start.10 = (f32[4,5,5]{2,1,0:T(8,128)S(1)}, f32[4,5,5]{2,1,0:T(8,128)}, u32[]{:S(2)}) copy-start(f32[4,5,5]{2,1,0:T(8,128)} %copy.105) | copy-start | bytes 1204
  32.3 1.1 %copy-start.11 = (f32[4,5,5]{2,1,0:T(8,128)S(1)}, f32[4,5,5]{2,1,0:T(8,128)}, u32[]{:S(2)}) copy-start(f32[4,5,5]{2,1,0:T(8,128)} %copy.103) | copy-start | bytes 1204
  32.3 1.1 %copy-start.12 = (f32[4,5,5]{2,1,0:T(8,128)S(1)}, f32[4,5,5]{2,1,0:T(8,128)}, u32[]{:S(2)}) copy-start(f32[4,5,5]{2,1,0:T(8,128)} %copy.101) | copy-start | bytes 1204
  32.3 1.1 %copy-start.13 = (f32[4,5,5]{2,1,0:T(8,128)S(1)}, f32[4,5,5]{2,1,0:T(8,128)}, u32[]{:S(2)}) copy-start(f32[4,5,5]{2,1,0:T(8,128)} %copy.99) | copy-start | bytes 1204
  32.3 1.1 %copy-start.14 = (f32[4,5,5]{2,1,0:T(8,128)S(1)}, f32[4,5,5]{2,1,0:T(8,128)}, u32[]{:S(2)}) copy-start(f32[4,5,5]{2,1,0:T(8,128)} %copy.97) | copy-start | bytes 1204
  32.3 1.1 %copy-start.15 = (f32[4,5,5]{2,1,0:T(8,128)S(1)}, f32[4,5,5]{2,1,0:T(8,128)}, u32[]{:S(2)}) copy-start(f32[4,5,5]{2,1,0:T(8,128)} %copy.95) | copy-start | bytes 1204
  32.3 1.1 %copy-start.16 = (f32[4,5,5]{2,1,0:T(8,128)S(1)}, f32[4,5,5]{2,1,0:T(8,128)}, u32[]{:S(2)}) copy-start(f32[4,5,5]{2,1,0:T(8,128)} %copy.93) | copy-start | bytes 1204
  33.4 3.2 %copy-start = (bf16[2,2,2,344,320]{3,4,2,1,0:T(8,128)(2,1)S(1)}, bf16[2,2,2,344,320]{3,4,2,1,0:T(8,128)(2,1)}, u32[]{:S(2)}) copy-start(bf16[2,2,2,344,320]{3,4,2,1,0:T(8,128)(2,1)} %param.4) | copy-start | bytes 5283844

commit v2 on v1

--- a/solution.py
+++ b/solution.py
@@ -21,42 +21,15 @@
 MESH = pl.DeviceIdType.MESH
 
 
-def halo(block, width, dim):
-    count = lax.axis_size("strip")
-    forward = [(i, i + 1) for i in range(count - 1)]
-    backward = [(target, source) for source, target in forward]
-    low = lax.ppermute(
-        lax.slice_in_dim(block, block.shape[dim] - width, None, axis=dim), "strip", forward
+def tap_weights(k, fraction):
+    distance = k.astype(jnp.float32) - (TAP_COUNT // 2 - 1) - fraction.astype(jnp.float32) / SUBSTEPS
+    angle = jnp.pi * distance
+    sinc = jnp.where(
+        distance == 0.0, 1.0, jnp.sin(angle) / jnp.where(distance == 0.0, 1.0, angle)
     )
-    high = lax.ppermute(lax.slice_in_dim(block, 0, width, axis=dim), "strip", backward)
-    return low, high
-
-
-def tap_weights(fraction_part):
-    offset = fraction_part.astype(jnp.float32) / SUBSTEPS
-    tap_axis = jnp.arange(TAP_COUNT).astype(jnp.float32)
-    distance = tap_axis - (TAP_COUNT // 2 - 1) - offset[..., None]
-    weights = jnp.sinc(distance) * (0.5 + 0.5 * jnp.cos(jnp.pi * distance / (TAP_COUNT // 2)))
-    return weights / jnp.sum(weights, axis=-1, keepdims=True)
-
-
-def tap_vectors(shifts, fractions):
-    weights = tap_weights(fractions)
-    first = shifts + (MARGIN - TAP_COUNT // 2 + 1)
-    base = (jnp.arange(shifts.shape[-1], dtype=jnp.int32) % 2) * CHIP_SIZE
-    lane = jnp.arange(LANES, dtype=jnp.int32)
-    lines = jnp.zeros(shifts.shape[1:] + (LANES,), jnp.float32)
-    columns = lines
-    for k in range(TAP_COUNT):
-        lines = lines + jnp.where(
-            lane == (first[0] + k)[..., None], weights[0, ..., k][..., None], 0.0
-        )
-        columns = columns + jnp.where(
-            lane == ((base - first[1] - k) % LANES)[..., None],
-            weights[1, ..., k][..., None],
-            0.0,
-        )
-    return lines, columns
+    weights = sinc * (0.5 + 0.5 * jnp.cos(jnp.pi * distance / (TAP_COUNT // 2)))
+    weights = jnp.where((k >= 0) & (k < TAP_COUNT), weights, 0.0)
+    return weights / jnp.sum(weights, axis=1, keepdims=True)
 
 
 def spread_rows(row, count):
@@ -73,18 +46,24 @@
 
 
 def kernel(
-    n, dims,
-    even_ref, odd_ref, lines_ref, cols_ref, cand_ref,
+    n, strips, dims,
+    frame_ref, shifts_ref, fractions_ref, dates_ref,
     coh_ref, sums_ref,
+    even_ref, odd_ref, lines_ref, cols_ref, cand_ref, edge_out, edge_in, picked, spots,
     series, sent, got, acc, part_buf, whole, looks, chip_rows, out_buf,
-    ref_send, ref_recv, next_send, next_recv, coh_send, coh_recv,
+    ref_send, ref_recv, next_send, next_recv, coh_send, coh_recv, edge_send, edge_recv,
 ):
     tiles, chips_az, chips_rg, rows, cols = dims
     me = lax.axis_index("date")
+    strip = lax.axis_index("strip")
     bits = n.bit_length() - 1
     groups = cand_ref.shape[0]
+    all_rows = rows + 2 * MARGIN
     blocks = series.shape[3]
     wide = blocks * LANES
+    kept_dates = series.shape[0] - 1
+    images = frame_ref.shape[0]
+    rest = cols - (blocks - 1) * LANES
     bf16 = jnp.bfloat16
     f32 = jnp.float32
 
@@ -93,7 +72,95 @@
         pl.semaphore_signal(
             barrier, inc=1, device_id={"date": lax.rem(me + o, n)}, device_id_type=MESH
         )
-    pl.semaphore_wait(barrier, n - 1)
+    has_low = strip > 0
+    has_high = strip < strips - 1
+
+    @pl.when(has_low)
+    def _():
+        pl.semaphore_signal(barrier, inc=1, device_id={"strip": strip - 1}, device_id_type=MESH)
+
+    @pl.when(has_high)
+    def _():
+        pl.semaphore_signal(barrier, inc=1, device_id={"strip": strip + 1}, device_id_type=MESH)
+
+    def for_rows(body):
+        count = all_rows // CHIP_SIZE
+
+        def step(i, carry):
+            body(pl.multiple_of(i * CHIP_SIZE, CHIP_SIZE), CHIP_SIZE)
+            return carry
+
+        lax.fori_loop(0, count, step, 0)
+        if all_rows > count * CHIP_SIZE:
+            body(count * CHIP_SIZE, all_rows - count * CHIP_SIZE)
+
+    def block_of(q, row, size, m):
+        width = min(LANES, cols - m * LANES)
+        value = frame_ref[q, pl.ds(row, size), m * LANES : m * LANES + width].astype(f32)
+        if width < LANES:
+            value = jnp.concatenate([value, jnp.zeros((size, LANES - width), f32)], axis=1)
+        return value
+
+    def pack_edges(row, size):
+        at = lax.broadcasted_iota(jnp.int32, (size, LANES), 1)
+        right = jnp.zeros((size, LANES), f32)
+        left = jnp.zeros((size, LANES), f32)
+        for q in range(images):
+            place = (at >= MARGIN * q) & (at < MARGIN * (q + 1))
+            last = block_of(q, row, size, blocks - 1)
+            first = block_of(q, row, size, 0)
+            last = pltpu.roll(last, (MARGIN * q - rest + MARGIN) % LANES, 1)
+            if q:
+                first = pltpu.roll(first, MARGIN * q, 1)
+            right = jnp.where(place, last, right)
+            left = jnp.where(place, first, left)
+        edge_out[0, pl.ds(row, size), :] = right.astype(bf16)
+        edge_out[1, pl.ds(row, size), :] = left.astype(bf16)
+
+    for_rows(pack_edges)
+
+    def pick_tile(tc, carry):
+        t = tc // 2
+        gains = [
+            jnp.where(dates_ref[t] == me * kept_dates + d, 1.0, 0.0).astype(f32)
+            for d in range(kept_dates)
+        ]
+
+        def select(row, size):
+            total = jnp.zeros((size, cols), f32)
+            for d in range(kept_dates):
+                image = frame_ref[d * tiles * 2 + tc, pl.ds(row, size), :]
+                total = total + image.astype(f32) * gains[d]
+            picked[pl.ds(row, size), :] = total
+
+        for_rows(select)
+        count = rows // GROUP
+        for g in range(count):
+            low = MARGIN + g * GROUP
+            cand_ref[tc * count + g] = picked[low : low + GROUP, :].astype(bf16)
+        return carry
+
+    lax.fori_loop(0, tiles * 2, pick_tile, 0)
+
+    beside = jnp.minimum(strip, 1) + jnp.minimum(strips - 1 - strip, 1)
+    pl.semaphore_wait(barrier, n - 1 + beside)
+
+    edges = [
+        pltpu.make_async_remote_copy(
+            src_ref=edge_out.at[i], dst_ref=edge_in.at[i],
+            send_sem=edge_send.at[i], recv_sem=edge_recv.at[i],
+            device_id={"strip": strip + 1 - 2 * i}, device_id_type=MESH,
+        )
+        for i in range(2)
+    ]
+
+    @pl.when(has_high)
+    def _():
+        edges[0].start()
+
+    @pl.when(has_low)
+    def _():
+        edges[1].start()
 
     offsets = [jnp.int32(0)]
     for b in range(bits):
@@ -172,8 +239,9 @@
                     r = 2 * m + side
                     if r >= chips_rg:
                         continue
-                    line_row = lines_ref[d * tiles + t, a, r : r + 1, :]
-                    col_row = cols_ref[d * tiles + t, a, r : r + 1, :]
+                    row_at = ((d * tiles + t) * chips_az + a) * chips_rg + r
+                    line_row = lines_ref[pl.ds(row_at, 1), :]
+                    col_row = cols_ref[pl.ds(row_at, 1), :]
                     line_mat = spread_rows(line_row, CHIP_SIZE).astype(bf16)[:, :window]
                     col_mat = spread_rows(col_row, LANES)
                     keep = lane < CHIP_SIZE if side == 0 else lane >= CHIP_SIZE
@@ -200,6 +268,73 @@
         lax.fori_loop(first, last, chip_line, 0)
 
     advance()
+
+    chip = 0
+    for d in range(kept_dates):
+        for t in range(tiles):
+            for a in range(chips_az):
+                for r in range(chips_rg):
+                    values = (
+                        shifts_ref[0, d, t, a, r] + (MARGIN - TAP_COUNT // 2 + 1),
+                        (r % 2) * CHIP_SIZE
+                        - shifts_ref[1, d, t, a, r]
+                        - (MARGIN - TAP_COUNT // 2 + 1),
+                        fractions_ref[0, d, t, a, r],
+                        fractions_ref[1, d, t, a, r],
+                    )
+                    for i, value in enumerate(values):
+                        spots[i, chip : chip + 1, :] = jnp.full((1, LANES), value, jnp.int32)
+                    chip += 1
+    at = lax.broadcasted_iota(jnp.int32, (chip, LANES), 1)
+    lines_ref[:chip] = tap_weights(at - spots[0, :chip], spots[2, :chip])
+    cols_ref[:chip] = tap_weights((spots[1, :chip] - at) & (LANES - 1), spots[3, :chip])
+
+    @pl.when(has_low)
+    def _():
+        edges[0].wait_recv()
+
+    @pl.when(has_high)
+    def _():
+        edges[1].wait_recv()
+
+    @pl.when(strip == 0)
+    def _():
+        edge_in[0] = jnp.zeros(edge_in.shape[1:], bf16)
+
+    @pl.when(strip == strips - 1)
+    def _():
+        edge_in[1] = jnp.zeros(edge_in.shape[1:], bf16)
+
+    advance()
+    tall = even_ref.shape[1]
+
+    def shift_image(q, carry):
+        def body(row, size):
+            at = lax.broadcasted_iota(jnp.int32, (size, LANES), 1)
+            low = edge_in[0, pl.ds(row, size), :].astype(f32)
+            high = edge_in[1, pl.ds(row, size), :].astype(f32)
+            low = pltpu.roll(low, lax.rem(LANES - MARGIN * q, LANES), 1)
+            high = pltpu.roll(high, lax.rem(2 * LANES + rest + MARGIN - MARGIN * q, LANES), 1)
+            moved = [pltpu.roll(block_of(q, row, size, m), MARGIN, 1) for m in range(blocks)]
+            even = [
+                jnp.where(at < MARGIN, low if m == 0 else moved[m - 1], moved[m])
+                for m in range(blocks)
+            ]
+            ends = (at >= rest + MARGIN) & (at < rest + 2 * MARGIN)
+            even[-1] = jnp.where(ends, high, even[-1])
+            half = [pltpu.roll(value, CHIP_SIZE, 1) for value in even]
+            for m in range(blocks):
+                even_ref[q, pl.ds(row, size), m * LANES : (m + 1) * LANES] = even[m].astype(bf16)
+            for m in range(chips_rg // 2):
+                value = jnp.where(at < CHIP_SIZE, half[m], half[m + 1])
+                odd_ref[q, pl.ds(row, size), m * LANES : (m + 1) * LANES] = value.astype(bf16)
+
+        for_rows(body)
+        even_ref[q, all_rows:, :] = jnp.zeros((tall - all_rows, wide), bf16)
+        odd_ref[q, all_rows:, :] = jnp.zeros((tall - all_rows, odd_ref.shape[2]), bf16)
+        return carry
+
+    lax.fori_loop(0, images, shift_image, 0)
     middle = (chips_az + 1) // 2
     last_d = series.shape[0] - 2
     following = [None]
@@ -355,37 +490,28 @@
     def _():
         following[0].wait_send()
 
-
-def per_device(n, acquisitions, shifts, fractions, ref_dates):
+    @pl.when(has_high)
+    def _():
+        edges[0].wait_send()
+
+    @pl.when(has_low)
+    def _():
+        edges[1].wait_send()
+
+
+def per_device(n, strips, acquisitions, shifts, fractions, ref_dates):
     dates_local, tiles, _, all_rows, cols = acquisitions.shape
     rows = all_rows - 2 * MARGIN
     chips_az, chips_rg = shifts.shape[3:]
-    wide = -(-cols // LANES) * LANES
-    low, high = halo(acquisitions, MARGIN, 4)
-    owners = ref_dates // dates_local
-    slots = ref_dates % dates_local
-    me = lax.axis_index("date")
-    cand = jnp.stack(
-        [
-            jnp.where(
-                owners[t] == me,
-                lax.dynamic_index_in_dim(acquisitions[:, t], slots[t], 0, keepdims=False)[
-                    :, MARGIN : MARGIN + rows, :
-                ],
-                0,
-            ).astype(acquisitions.dtype)
-            for t in range(tiles)
-        ]
-    ).reshape(tiles * 2 * rows // GROUP, GROUP, cols)
-    padded = jnp.concatenate([low, acquisitions, high], axis=4)
-    flat = padded.reshape((-1,) + padded.shape[3:])
+    blocks = -(-cols // LANES)
+    wide = blocks * LANES
+    images = dates_local * tiles * 2
+    frames = acquisitions.reshape(images, all_rows, cols)
     tall = -(-all_rows // 32) * 32
-    even = jnp.pad(flat, ((0, 0), (0, tall - all_rows), (0, wide - flat.shape[2])))
     odd_wide = (chips_rg // 2) * LANES
-    odd = even[:, :, CHIP_SIZE : CHIP_SIZE + odd_wide]
-    lines, columns = tap_vectors(shifts, fractions)
-    lines = lines.reshape((-1,) + lines.shape[2:])
-    columns = columns.reshape((-1,) + columns.shape[2:])
+    chips = dates_local * tiles * chips_az * chips_rg
+    chips_tall = -(-chips // GROUP) * GROUP
+    groups = tiles * 2 * rows // GROUP
 
     look_rows = rows // LOOK_AZ
     looks_rg = cols // LOOK_RG
@@ -395,17 +521,25 @@
     vmem = pl.BlockSpec(memory_space=pltpu.VMEM)
     f32 = jnp.float32
     bf16 = jnp.bfloat16
-    groups = cand.shape[0]
     dma = pltpu.SemaphoreType.DMA
     coh, sums = pl.pallas_call(
-        functools.partial(kernel, n, (tiles, chips_az, chips_rg, rows, cols)),
+        functools.partial(kernel, n, strips, (tiles, chips_az, chips_rg, rows, cols)),
         out_shape=(
             jax.ShapeDtypeStruct((n, share, LANES), f32),
             jax.ShapeDtypeStruct((tiles, chips_az, stat_rows, LANES), f32),
         ),
-        in_specs=[vmem] * 5,
+        in_specs=[vmem] + [pl.BlockSpec(memory_space=pltpu.SMEM)] * 3,
         out_specs=(vmem, vmem),
         scratch_shapes=[
+            pltpu.VMEM((images, tall, wide), bf16),
+            pltpu.VMEM((images, tall, odd_wide), bf16),
+            pltpu.VMEM((chips_tall, LANES), f32),
+            pltpu.VMEM((chips_tall, LANES), f32),
+            pltpu.VMEM((groups, GROUP, cols), bf16),
+            pltpu.VMEM((2, all_rows, LANES), bf16),
+            pltpu.VMEM((2, all_rows, LANES), bf16),
+            pltpu.VMEM((all_rows, cols), f32),
+            pltpu.VMEM((4, chips_tall, LANES), jnp.int32),
             pltpu.VMEM((dates_local + 1, tiles, 2, wide // LANES, rows, LANES), f32),
             pltpu.VMEM((tiles, 2, wide // LANES, rows, LANES), bf16),
             pltpu.VMEM((tiles, 2, wide // LANES, rows, LANES), bf16),
@@ -416,11 +550,12 @@
             pltpu.VMEM((tiles, chips_az, stat_rows, cols), f32),
             pltpu.VMEM((n, share, LANES), f32),
             dma((2 * bits,)), dma((2 * bits,)), dma, dma, dma((n,)), dma((n,)),
+            dma((2,)), dma((2,)),
         ],
         compiler_params=pltpu.CompilerParams(
             collective_id=0, has_side_effects=True, vmem_limit_bytes=50 * 1024 * 1024
         ),
-    )(even, odd, lines, columns, cand)
+    )(frames, shifts, fractions, ref_dates)
 
     stats = sums[..., :chips_rg]
     ref_power = stats[:, :, 0]
@@ -435,7 +570,7 @@
 
 def solution(mesh):
     return jax.shard_map(
-        functools.partial(per_device, mesh.shape["date"]),
+        functools.partial(per_device, mesh.shape["date"], mesh.shape["strip"]),
         mesh=mesh,
         in_specs=(
             P("date", None, None, None, "strip"),

time: 97.5 us -> 64.5 us (0.66)
  local copies, waits for them, and re-layouts: 21.7 us -> 6.42 us
  other arithmetic: 12.2 us -> 0.04 us
  starting transfers between devices: 6.17 us -> 0 us
  Pallas kernels: 50.9 us -> 57 us
  between operations: 6.17 us -> 0.73 us
    ppermute x2 -> x0, starting transfers between devices: 6.17 us -> none  [the longest x1 4.88 us: halo(): lax.ppermute(lax.slice_in_dim(block, block.shape[dim] - width, None, axis...]
    pallas_call x1, Pallas kernels: 50.9 us -> 57 us  [per_device(): pl.pallas_call(functools.partial(kernel, n, strips, (tiles, chips_az, chi...]
    broadcast_in_dim x16 -> x0, local copies, waits for them, and re-layouts: 4.84 us -> none  [the longest x8 4.81 us: tap_vectors(): jnp.where(lane == (first[0] + k)[..., None], weights[0, ..., k][..., None...]
    unnamed x36 -> x7, local copies, waits for them, and re-layouts: 1.51 us -> 5.87 us
    slice x8 -> x0, local copies, waits for them, and re-layouts: 4.23 us -> none  [the longest x1 1.7 us: per_device(): acquisitions[:, t]]
    add x7 -> x0, local copies, waits for them, and re-layouts: 4.21 us -> none  [tap_vectors(): first[0] + k]
    reduce_sum x1 -> x0, other arithmetic: 3.21 us -> none  [tap_weights(): return weights / jnp.sum(weights, axis=-1, keepdims=True)]
    div x1 -> x0, other arithmetic: 3.13 us -> none  [tap_weights(): return weights / jnp.sum(weights, axis=-1, keepdims=True)]
  transfers between devices with their start and end apart: 2 -> 0, of which waited for: 0 -> 0; matrix products, arithmetic and copies ran while one was open for 24% -> 0% of each run, Pallas kernels for 0% -> 0%
where the time goes in v2:
time: 64.5 us; the launch traced here: 64.2 us
  Pallas kernels  57 us (88%)
  local copies, waits for them, and re-layouts  6.42 us (10%)
  between operations  0.73 us (1%)
    pallas_call x1, Pallas kernels, per_device(): pl.pallas_call(functools.partial(kernel, n, strips, (tiles, chips_az, chi...  57 us
    unnamed x7, local copies, waits for them, and re-layouts  5.87 us

profile of v2, /device:TPU:0, one launch (start us, length us, event | category | flops | bytes accessed | tf_op | source)
XLA Modules:
  0.0 64.2 jit_solution(4027693832551938659)
XLA Ops:
  0.6 0.0 copy-start
  0.6 0.7 %copy.23.shifts_ref = s32[2,2,2,5,5]{4,3,2,1,0:T(8,128)S(1)} copy(s32[2,2,2,5,5]{4,2,3,1,0:T(2,128)} %param.5) | data formatting | bytes 1600 | tf_op args[1]
  1.4 0.7 %copy.24.fractions_ref = s32[2,2,2,5,5]{4,3,2,1,0:T(8,128)S(1)} copy(s32[2,2,2,5,5]{4,2,3,1,0:T(2,128)} %param.6) | data formatting | bytes 1600 | tf_op args[2]
  2.1 3.0 %copy.22 = bf16[2,2,2,344,320]{4,3,2,1,0:T(8,128)(2,1)S(1)} copy(bf16[2,2,2,344,320]{3,4,2,1,0:T(8,128)(2,1)} %param.4) | data formatting | bytes 3522560 | tf_op args[0]
  5.1 0.0 copy-done
  5.1 57.0 %shard_map.59 = (f32[16,4,128]{2,1,0:T(4,128)S(1)}, f32[2,5,7,128]{3,2,1,0:T(8,128)S(1)}) custom-call(bf16[8,344,320]{2,1,0:T(8,128)(2,1)S(1)} %bitcast.13, s32[2,2,2,5,5]{4,3,2,1,0:T(8,128)S(1)} %copy.23.shifts_ref, s32[2,2,2,5,5]{4,3,2,1,0:T(8,128)S(1)} %copy.24.fractions_ref, s32[2]{0:T(128)S(1)} %copy-done), custom_call_target="tpu_custom_call" | custom-call | tf_op jit(solution)/shard_map/pallas_call | solution.py:525
  62.2 0.6 copy.31
  62.8 0.4 reshape.27
  63.2 0.1 copy.30
  63.4 0.8 %copy.32 = f32[2,31,2,4,16]{1,4,3,2,0:T(8,128)} copy(f32[2,31,2,4,16]{4,1,3,2,0:T(8,128)S(1)} %bitcast.14) | data formatting | bytes 63488
  (6 shorter events, 0.1 us)
Async XLA Ops:
  0.6 4.5 %copy-start = (s32[2]{0:T(128)S(1)}, s32[2]{0:T(128)}, u32[]{:S(2)}) copy-start(s32[2]{0:T(128)} %dates_ref.1) | copy-start | bytes 28

commit v3 on v2

--- a/solution.py
+++ b/solution.py
@@ -47,9 +47,9 @@
 
 def kernel(
     n, strips, dims,
-    frame_ref, shifts_ref, fractions_ref, dates_ref,
+    frame_hbm, shifts_ref, fractions_ref, dates_ref,
     coh_ref, sums_ref,
-    even_ref, odd_ref, lines_ref, cols_ref, cand_ref, edge_out, edge_in, picked, spots,
+    frame_ref, frame_sem, even_ref, odd_ref, lines_ref, cols_ref, cand_ref, edge_out, edge_in, picked, spots,
     series, sent, got, acc, part_buf, whole, looks, chip_rows, out_buf,
     ref_send, ref_recv, next_send, next_recv, coh_send, coh_recv, edge_send, edge_recv,
 ):
@@ -57,7 +57,7 @@
     me = lax.axis_index("date")
     strip = lax.axis_index("strip")
     bits = n.bit_length() - 1
-    groups = cand_ref.shape[0]
+    groups = cand_ref.shape[1]
     all_rows = rows + 2 * MARGIN
     blocks = series.shape[3]
     wide = blocks * LANES
@@ -67,6 +67,8 @@
     bf16 = jnp.bfloat16
     f32 = jnp.float32
 
+    load = pltpu.make_async_copy(frame_hbm, frame_ref, frame_sem)
+    load.start()
     barrier = pltpu.get_barrier_semaphore()
     for o in range(1, n):
         pl.semaphore_signal(
@@ -117,6 +119,7 @@
         edge_out[0, pl.ds(row, size), :] = right.astype(bf16)
         edge_out[1, pl.ds(row, size), :] = left.astype(bf16)
 
+    load.wait()
     for_rows(pack_edges)
 
     def pick_tile(tc, carry):
@@ -137,7 +140,7 @@
         count = rows // GROUP
         for g in range(count):
             low = MARGIN + g * GROUP
-            cand_ref[tc * count + g] = picked[low : low + GROUP, :].astype(bf16)
+            cand_ref[t, (tc % 2) * count + g] = picked[low : low + GROUP, :].astype(bf16)
         return carry
 
     lax.fori_loop(0, tiles * 2, pick_tile, 0)
@@ -162,66 +165,71 @@
     def _():
         edges[1].start()
 
-    offsets = [jnp.int32(0)]
-    for b in range(bits):
-        offsets.append(offsets[-1] + ((me // (1 << b)) % 2) * (groups >> (b + 1)))
+    orders = [list(range(bits))]
+    for t in range(1, tiles):
+        orders.append([0] + list(range(2, bits)) + [1] if bits > 2 else orders[0])
+    offsets = []
+    for order in orders:
+        offset = [jnp.int32(0)]
+        for s, b in enumerate(order):
+            offset.append(offset[-1] + ((me // (1 << b)) % 2) * (groups >> (s + 1)))
+        offsets.append(offset)
 
     def partner(b):
         return me + (1 - 2 * ((me // (1 << b)) % 2)) * (1 << b)
 
-    def halving(b):
-        half = groups >> (b + 1)
-        away = offsets[b] + (1 - (me // (1 << b)) % 2) * half
-        source = cand_ref if b == 0 else acc
+    def halving(t, s):
+        b = orders[t][s]
+        half = groups >> (s + 1)
+        away = offsets[t][s] + (1 - (me // (1 << b)) % 2) * half
+        source = cand_ref if s == 0 else acc
         return pltpu.make_async_remote_copy(
-            src_ref=source.at[pl.ds(away, half)],
-            dst_ref=part_buf.at[pl.ds(groups - 2 * half, half)],
-            send_sem=ref_send.at[b],
-            recv_sem=ref_recv.at[b],
+            src_ref=source.at[t, pl.ds(away, half)],
+            dst_ref=part_buf.at[t, pl.ds(groups - 2 * half, half)],
+            send_sem=ref_send.at[t, s],
+            recv_sem=ref_recv.at[t, s],
             device_id={"date": partner(b)},
             device_id_type=MESH,
         )
 
-    def add_half(b):
-        half = groups >> (b + 1)
-        source = cand_ref if b == 0 else acc
-        target = whole if b == bits - 1 else acc
-
-        def body(i, carry):
-            g = offsets[b + 1] + i
-            target[g] = source[g] + part_buf[groups - 2 * half + i]
-            return carry
-
-        lax.fori_loop(0, half, body, 0)
-
-    def doubling(b):
-        half = groups >> (b + 1)
-        mine = whole.at[pl.ds(offsets[b + 1], half)]
+    def add_half(t, s):
+        half = groups >> (s + 1)
+        source = cand_ref if s == 0 else acc
+        target = whole if s == bits - 1 else acc
+        at = pl.ds(offsets[t][s + 1], half)
+        target[t, at] = source[t, at] + part_buf[t, groups - 2 * half : groups - half]
+
+    def doubling(t, s):
+        half = groups >> (s + 1)
+        mine = whole.at[t, pl.ds(offsets[t][s + 1], half)]
         return pltpu.make_async_remote_copy(
             src_ref=mine,
             dst_ref=mine,
-            send_sem=ref_send.at[bits + b],
-            recv_sem=ref_recv.at[bits + b],
-            device_id={"date": partner(b)},
+            send_sem=ref_send.at[t, bits + s],
+            recv_sem=ref_recv.at[t, bits + s],
+            device_id={"date": partner(orders[t][s])},
             device_id_type=MESH,
         )
 
-    state = {"step": 0, "copy": None}
+    state = {"step": 0, "copies": None}
 
     def advance():
         step = state["step"]
         if step > 2 * bits:
             return
-        if step > 0:
-            state["copy"].wait()
-            if step <= bits:
-                add_half(step - 1)
-        if step < bits:
-            state["copy"] = halving(step)
-            state["copy"].start()
-        elif step < 2 * bits:
-            state["copy"] = doubling(2 * bits - 1 - step)
-            state["copy"].start()
+        sent_now = []
+        for t in range(tiles):
+            if step > 0:
+                state["copies"][t].wait()
+                if step <= bits:
+                    add_half(t, step - 1)
+            if step < bits:
+                sent_now.append(halving(t, step))
+                sent_now[-1].start()
+            elif step < 2 * bits:
+                sent_now.append(doubling(t, 2 * bits - 1 - step))
+                sent_now[-1].start()
+        state["copies"] = sent_now
         state["step"] = step + 1
 
     lane = lax.broadcasted_iota(jnp.int32, (LANES, LANES), 1)
@@ -308,41 +316,58 @@
     advance()
     tall = even_ref.shape[1]
 
+    def picker(depth, width, want):
+        source = lax.broadcasted_iota(jnp.int32, (depth, width), 0)
+        at = lax.broadcasted_iota(jnp.int32, (depth, width), 1)
+        return jnp.where(source == want(at), 1.0, 0.0).astype(bf16)
+
+    def moved(values, matrix):
+        return jnp.dot(values, matrix, preferred_element_type=f32).astype(bf16)
+
+    both_move = picker(
+        2 * LANES,
+        2 * LANES,
+        lambda at: jnp.where(at < LANES, at + LANES - MARGIN, at - LANES + CHIP_SIZE - MARGIN),
+    )
+    first_move = picker(LANES, LANES, lambda at: at - MARGIN)
+    row_cut = (all_rows // 2 + 15) // 16 * 16
+
     def shift_image(q, carry):
-        def body(row, size):
-            at = lax.broadcasted_iota(jnp.int32, (size, LANES), 1)
-            low = edge_in[0, pl.ds(row, size), :].astype(f32)
-            high = edge_in[1, pl.ds(row, size), :].astype(f32)
-            low = pltpu.roll(low, lax.rem(LANES - MARGIN * q, LANES), 1)
-            high = pltpu.roll(high, lax.rem(2 * LANES + rest + MARGIN - MARGIN * q, LANES), 1)
-            moved = [pltpu.roll(block_of(q, row, size, m), MARGIN, 1) for m in range(blocks)]
-            even = [
-                jnp.where(at < MARGIN, low if m == 0 else moved[m - 1], moved[m])
-                for m in range(blocks)
-            ]
-            ends = (at >= rest + MARGIN) & (at < rest + 2 * MARGIN)
-            even[-1] = jnp.where(ends, high, even[-1])
-            half = [pltpu.roll(value, CHIP_SIZE, 1) for value in even]
-            for m in range(blocks):
-                even_ref[q, pl.ds(row, size), m * LANES : (m + 1) * LANES] = even[m].astype(bf16)
-            for m in range(chips_rg // 2):
-                value = jnp.where(at < CHIP_SIZE, half[m], half[m + 1])
-                odd_ref[q, pl.ds(row, size), m * LANES : (m + 1) * LANES] = value.astype(bf16)
-
-        for_rows(body)
+        low_move = picker(LANES, LANES, lambda at: jnp.where(at < MARGIN, at + MARGIN * q, -1))
+        skip = rest + MARGIN
+        high_move = picker(
+            LANES,
+            LANES,
+            lambda at: jnp.where(
+                (at >= skip) & (at < skip + MARGIN), at - skip + MARGIN * q, -1
+            ),
+        )
+        for row, size in ((0, row_cut), (row_cut, all_rows - row_cut)):
+            span = slice(row, row + size)
+            even_ref[q, span, :LANES] = moved(frame_ref[q, span, :LANES], first_move) + moved(
+                edge_in[0, span, :], low_move
+            )
+            for m in range(blocks - 1):
+                width = min(2 * LANES, cols - m * LANES)
+                pair = moved(
+                    frame_ref[q, span, m * LANES : m * LANES + width], both_move[:width]
+                )
+                block = pair[:, :LANES]
+                if m == blocks - 2:
+                    block = block + moved(edge_in[1, span, :], high_move)
+                even_ref[q, span, (m + 1) * LANES : (m + 2) * LANES] = block
+                odd_ref[q, span, m * LANES : (m + 1) * LANES] = pair[:, LANES:]
         even_ref[q, all_rows:, :] = jnp.zeros((tall - all_rows, wide), bf16)
         odd_ref[q, all_rows:, :] = jnp.zeros((tall - all_rows, odd_ref.shape[2]), bf16)
         return carry
 
     lax.fori_loop(0, images, shift_image, 0)
-    middle = (chips_az + 1) // 2
     last_d = series.shape[0] - 2
     following = [None]
     for d in range(last_d + 1):
         for t in range(tiles):
-            resample(d, t, 0, middle)
             advance()
-            resample(d, t, middle, chips_az)
+            resample(d, t, 0, chips_az)
             if d == 0 and t == tiles - 1:
                 following[0] = pltpu.make_async_remote_copy(
                     src_ref=sent, dst_ref=got, send_sem=next_send, recv_sem=next_recv,
@@ -460,8 +485,8 @@
                 total = [jnp.zeros((GROUP, size), f32)] * (1 + 3 * kept)
                 for g in range(line_groups):
                     at = a * line_groups + g
-                    rr = whole[(t * 2) * (rows // GROUP) + at, :, span].astype(f32)
-                    ri = whole[(t * 2 + 1) * (rows // GROUP) + at, :, span].astype(f32)
+                    rr = whole[t, at, :, span].astype(f32)
+                    ri = whole[t, rows // GROUP + at, :, span].astype(f32)
                     total[0] = total[0] + (rr * rr + ri * ri)
                     row = pl.multiple_of(at * GROUP, GROUP)
                     for d in range(kept):
@@ -511,7 +536,7 @@
     odd_wide = (chips_rg // 2) * LANES
     chips = dates_local * tiles * chips_az * chips_rg
     chips_tall = -(-chips // GROUP) * GROUP
-    groups = tiles * 2 * rows // GROUP
+    groups = -(-(2 * rows // GROUP) // n) * n
 
     look_rows = rows // LOOK_AZ
     looks_rg = cols // LOOK_RG
@@ -528,14 +553,16 @@
             jax.ShapeDtypeStruct((n, share, LANES), f32),
             jax.ShapeDtypeStruct((tiles, chips_az, stat_rows, LANES), f32),
         ),
-        in_specs=[vmem] + [pl.BlockSpec(memory_space=pltpu.SMEM)] * 3,
+        in_specs=[pl.BlockSpec(memory_space=pl.ANY)] + [pl.BlockSpec(memory_space=pltpu.SMEM)] * 3,
         out_specs=(vmem, vmem),
         scratch_shapes=[
+            pltpu.VMEM((images, all_rows, cols), bf16),
+            dma,
             pltpu.VMEM((images, tall, wide), bf16),
             pltpu.VMEM((images, tall, odd_wide), bf16),
             pltpu.VMEM((chips_tall, LANES), f32),
             pltpu.VMEM((chips_tall, LANES), f32),
-            pltpu.VMEM((groups, GROUP, cols), bf16),
+            pltpu.VMEM((tiles, groups, GROUP, cols), bf16),
             pltpu.VMEM((2, all_rows, LANES), bf16),
             pltpu.VMEM((2, all_rows, LANES), bf16),
             pltpu.VMEM((all_rows, cols), f32),
@@ -543,13 +570,13 @@
             pltpu.VMEM((dates_local + 1, tiles, 2, wide // LANES, rows, LANES), f32),
             pltpu.VMEM((tiles, 2, wide // LANES, rows, LANES), bf16),
             pltpu.VMEM((tiles, 2, wide // LANES, rows, LANES), bf16),
-            pltpu.VMEM((groups, GROUP, cols), bf16),
-            pltpu.VMEM((groups, GROUP, cols), bf16),
-            pltpu.VMEM((groups, GROUP, cols), bf16),
+            pltpu.VMEM((tiles, groups, GROUP, cols), bf16),
+            pltpu.VMEM((tiles, groups, GROUP, cols), bf16),
+            pltpu.VMEM((tiles, groups, GROUP, cols), bf16),
             pltpu.VMEM((tiles, dates_local + 1 + 2 * dates_local, look_rows, wide), f32),
             pltpu.VMEM((tiles, chips_az, stat_rows, cols), f32),
             pltpu.VMEM((n, share, LANES), f32),
-            dma((2 * bits,)), dma((2 * bits,)), dma, dma, dma((n,)), dma((n,)),
+            dma((tiles, 2 * bits)), dma((tiles, 2 * bits)), dma, dma, dma((n,)), dma((n,)),
             dma((2,)), dma((2,)),
         ],
         compiler_params=pltpu.CompilerParams(

time: 64.5 us -> 59.5 us (0.922)
  Pallas kernels: 57 us -> 52 us
    pallas_call x1, Pallas kernels: 57 us -> 52 us  [per_device(): pl.pallas_call(functools.partial(kernel, n, strips, (tiles, chips_az, chi...]
where the time goes in v3:
time: 59.5 us; the launch traced here: 59.2 us
  Pallas kernels  52 us (87%)
  local copies, waits for them, and re-layouts  6.42 us (11%)
  between operations  0.73 us (1%)
    pallas_call x1, Pallas kernels, per_device(): pl.pallas_call(functools.partial(kernel, n, strips, (tiles, chips_az, chi...  52 us
    unnamed x7, local copies, waits for them, and re-layouts  5.87 us

profile of v3, /device:TPU:0, one launch (start us, length us, event | category | flops | bytes accessed | tf_op | source)
XLA Modules:
  0.0 59.2 jit_solution(359961452608288278)
XLA Ops:
  0.6 0.0 copy-start
  0.6 0.7 %copy.23.shifts_ref = s32[2,2,2,5,5]{4,3,2,1,0:T(8,128)S(1)} copy(s32[2,2,2,5,5]{4,2,3,1,0:T(2,128)} %param.5) | data formatting | bytes 1600 | tf_op args[1]
  1.4 0.7 %copy.24.fractions_ref = s32[2,2,2,5,5]{4,3,2,1,0:T(8,128)S(1)} copy(s32[2,2,2,5,5]{4,2,3,1,0:T(2,128)} %param.6) | data formatting | bytes 1600 | tf_op args[2]
  2.1 3.0 %copy.22 = bf16[2,2,2,344,320]{4,3,2,1,0:T(8,128)(2,1)S(1)} copy(bf16[2,2,2,344,320]{3,4,2,1,0:T(8,128)(2,1)} %param.4) | data formatting | bytes 3522560 | tf_op args[0]
  5.1 0.0 copy-done
  5.1 52.0 %shard_map.59 = (f32[16,4,128]{2,1,0:T(4,128)S(1)}, f32[2,5,7,128]{3,2,1,0:T(8,128)S(1)}) custom-call(bf16[8,344,320]{2,1,0:T(8,128)(2,1)S(1)} %bitcast.13, s32[2,2,2,5,5]{4,3,2,1,0:T(8,128)S(1)} %copy.23.shifts_ref, s32[2,2,2,5,5]{4,3,2,1,0:T(8,128)S(1)} %copy.24.fractions_ref, s32[2]{0:T(128)S(1)} %copy-done), custom_call_target="tpu_custom_call" | custom-call | tf_op jit(solution)/shard_map/pallas_call | solution.py:550
  57.2 0.6 %copy.31 = f32[2,2,2,5,5]{4,2,3,1,0:T(2,128)} copy(f32[2,2,2,5,5]{4,2,0,1,3:T(2,128)S(1)} %slice_divide_fusion) | data formatting | bytes 1600
  57.9 0.4 reshape.27
  58.2 0.1 copy.30
  58.4 0.8 %copy.32 = f32[2,31,2,4,16]{1,4,3,2,0:T(8,128)} copy(f32[2,31,2,4,16]{4,1,3,2,0:T(8,128)S(1)} %bitcast.14) | data formatting | bytes 63488
  (6 shorter events, 0.1 us)
Async XLA Ops:
  0.6 4.5 %copy-start = (s32[2]{0:T(128)S(1)}, s32[2]{0:T(128)}, u32[]{:S(2)}) copy-start(s32[2]{0:T(128)} %dates_ref.1) | copy-start | bytes 28

commit v4 on v3

--- a/solution.py
+++ b/solution.py
@@ -377,6 +377,8 @@
                 @pl.when(me > 0)
                 def _():
                     following[0].start()
+
+    advance()
 
     @pl.when(me < n - 1)
     def _():

time: 59.5 us -> 60.7 us (1.020)
  Pallas kernels: 52 us -> 53.2 us
    pallas_call x1, Pallas kernels: 52 us -> 53.2 us  [per_device(): pl.pallas_call(functools.partial(kernel, n, strips, (tiles, chips_az, chi...]
where the time goes in v4:
time: 60.7 us; the launch traced here: 60.4 us
  Pallas kernels  53.2 us (88%)
  local copies, waits for them, and re-layouts  6.42 us (11%)
  between operations  0.73 us (1%)
    pallas_call x1, Pallas kernels, per_device(): pl.pallas_call(functools.partial(kernel, n, strips, (tiles, chips_az, chi...  53.2 us
    unnamed x7, local copies, waits for them, and re-layouts  5.87 us

profile of v4, /device:TPU:0, one launch (start us, length us, event | category | flops | bytes accessed | tf_op | source)
XLA Modules:
  0.0 60.4 jit_solution(13471043382976707794)
XLA Ops:
  0.6 0.0 copy-start
  0.6 0.7 %copy.23.shifts_ref = s32[2,2,2,5,5]{4,3,2,1,0:T(8,128)S(1)} copy(s32[2,2,2,5,5]{4,2,3,1,0:T(2,128)} %param.5) | data formatting | bytes 1600 | tf_op args[1]
  1.4 0.7 %copy.24.fractions_ref = s32[2,2,2,5,5]{4,3,2,1,0:T(8,128)S(1)} copy(s32[2,2,2,5,5]{4,2,3,1,0:T(2,128)} %param.6) | data formatting | bytes 1600 | tf_op args[2]
  2.1 3.0 %copy.22 = bf16[2,2,2,344,320]{4,3,2,1,0:T(8,128)(2,1)S(1)} copy(bf16[2,2,2,344,320]{3,4,2,1,0:T(8,128)(2,1)} %param.4) | data formatting | bytes 3522560 | tf_op args[0]
  5.1 0.0 copy-done
  5.1 53.2 %shard_map.59 = (f32[16,4,128]{2,1,0:T(4,128)S(1)}, f32[2,5,7,128]{3,2,1,0:T(8,128)S(1)}) custom-call(bf16[8,344,320]{2,1,0:T(8,128)(2,1)S(1)} %bitcast.13, s32[2,2,2,5,5]{4,3,2,1,0:T(8,128)S(1)} %copy.23.shifts_ref, s32[2,2,2,5,5]{4,3,2,1,0:T(8,128)S(1)} %copy.24.fractions_ref, s32[2]{0:T(128)S(1)} %copy-done), custom_call_target="tpu_custom_call" | custom-call | tf_op jit(solution)/shard_map/pallas_call | solution.py:552
  58.4 0.6 %copy.31 = f32[2,2,2,5,5]{4,2,3,1,0:T(2,128)} copy(f32[2,2,2,5,5]{4,2,0,1,3:T(2,128)S(1)} %slice_divide_fusion) | data formatting | bytes 1600
  59.0 0.4 reshape.27
  59.4 0.1 copy.30
  59.6 0.8 %copy.32 = f32[2,31,2,4,16]{1,4,3,2,0:T(8,128)} copy(f32[2,31,2,4,16]{4,1,3,2,0:T(8,128)S(1)} %bitcast.14) | data formatting | bytes 63488
  (6 shorter events, 0.1 us)
Async XLA Ops:
  0.6 4.5 %copy-start = (s32[2]{0:T(128)S(1)}, s32[2]{0:T(128)}, u32[]{:S(2)}) copy-start(s32[2]{0:T(128)} %dates_ref.1) | copy-start | bytes 28
